TPU v7x, 512 devices: a whole 4x8x8 slice. The times are simulated.
512 devices in a mesh: fsdp: 64 (over y, x, core), cent: 8 (over z).
Axes of the slice: x: 4, y: 8, z: 8, core: 2. Of those that a mesh axis runs over, the one named last changes fastest.
Arguments:
- attention: bfloat16 [8192, 4096], P('fsdp', 'cent'), may hold values from -6 to 6
- w_out: bfloat16 [4096, 4096], P('cent', 'fsdp'), may hold values from -0.09375 to 0.09375
- hidden: bfloat16 [8192, 4096], P(('fsdp', 'cent')), may hold values from -6 to 6
- norm_gain: bfloat16 [4096], replicated, may hold values from 0.099609375 to 1.8984375
- centroids: bfloat16 [512, 4096], P('cent'), may hold values from -3 to 3
- token_codes: int32 [8192], P(('fsdp', 'cent')), may hold values from 0 to 63, as said below
- tile_lists: int32 [64, 8], P('fsdp'), may hold values from 0 to 63, as said below
Outputs:
- centroid_sums: float32 [512, 4096], P('cent', 'fsdp')
- residual_gram: float32 [4096, 4096], P('fsdp', 'cent')
Inputs may be any that keep to these rules, and one draw needn't show every extreme that they name: `token_codes`: token t belongs to block t // 128; its code k names centroid k % 8 of the tile at slot k // 8 of that block's list; every slot of a block's list is used. `tile_lists`: each row holds 8 distinct tile ids in ascending order; tile j holds centroids j * 8 to j * 8 + 7, and centroid g belongs to owner shard g // 64; in every row at most 2 listed tiles share an owner, and exactly 2 do for some owner.
All inputs are finite; a program needn't handle non-finite values.
Results may differ from a plain program's by a relative error of at most 0.0085.
Values may be sent and summed in bfloat16 or wider, within the bound.
A program may use at most 64 MiB of HBM per device.

v0:
```python
import jax
import jax.numpy as jnp
from jax import lax
from jax.sharding import PartitionSpec as P

TILE = 8
LT = 8


def shards(attention, w_out, hidden, norm_gain, centroids, token_codes, tile_lists):
    tok_dev = hidden.shape[0]
    feat_dim = hidden.shape[1]
    n_fsdp = lax.axis_size("fsdp")
    n_cent = lax.axis_size("cent")
    cap_slots = max(2, 2 * LT // n_cent)
    partial_out = jnp.dot(
        attention,
        lax.all_gather(w_out, "fsdp", axis=1, tiled=True),
        preferred_element_type=jnp.float32,
    )
    head_sum = lax.psum_scatter(
        partial_out.astype(jnp.bfloat16), "cent", scatter_dimension=0, tiled=True
    ).astype(jnp.float32)
    mixed_rows = hidden.astype(jnp.float32) + head_sum
    normed = (
        mixed_rows
        * lax.rsqrt(jnp.mean(mixed_rows * mixed_rows, axis=1, keepdims=True) + 1e-05)
        * norm_gain.astype(jnp.float32)
    )
    cent_dev = centroids.shape[0]
    own_tiles = cent_dev // TILE
    owner_idx = lax.axis_index("cent")
    listed = tile_lists[0]
    local_tile = listed - owner_idx * own_tiles
    owned_here = (local_tile >= 0) & (local_tile < own_tiles)
    safe_tile = jnp.clip(local_tile, 0, own_tiles - 1)
    tiles_here = centroids.reshape(own_tiles, TILE, feat_dim)
    slot_of = token_codes // TILE
    offset = token_codes % TILE
    rank_mine = jnp.cumsum(owned_here.astype(jnp.int32)) - 1
    chosen = owned_here[None, :] & (
        rank_mine[None, :] == jnp.arange(cap_slots, dtype=jnp.int32)[:, None]
    )
    send_tile = jnp.sum(jnp.where(chosen, safe_tile[None, :], 0), axis=1)
    filled = jnp.any(chosen, axis=1)
    outgoing = jnp.where(
        filled[:, None, None],
        jnp.take(tiles_here, send_tile, axis=0),
        jnp.zeros((cap_slots, TILE, feat_dim), jnp.bfloat16),
    )
    arrived = lax.all_gather(outgoing, "cent", axis=0, tiled=True)
    owner_of = listed // own_tiles
    list_pos = jnp.arange(LT, dtype=jnp.int32)
    earlier = (owner_of[None, :] == owner_of[:, None]) & (list_pos[None, :] < list_pos[:, None])
    rank_all = jnp.sum(earlier.astype(jnp.int32), axis=1)
    where_tile = owner_of * cap_slots + rank_all
    tile_rows = arrived.reshape(-1, feat_dim)
    centers = jnp.take(tile_rows, where_tile[slot_of] * TILE + offset, axis=0)
    residual = (normed - centers.astype(jnp.float32)).astype(jnp.bfloat16)
    onehot = (token_codes[None, :] == jnp.arange(LT * TILE, dtype=jnp.int32)[:, None]).astype(
        jnp.bfloat16
    )
    slot_part = jnp.dot(onehot, residual, preferred_element_type=jnp.float32)
    slot_sum = lax.psum(slot_part.astype(jnp.bfloat16), "cent").astype(jnp.float32)
    target = (local_tile[:, None] * TILE + jnp.arange(TILE, dtype=jnp.int32)[None, :]).reshape(-1)
    valid_rows = jnp.repeat(owned_here, TILE)
    placer = (
        (jnp.arange(cent_dev, dtype=jnp.int32)[:, None] == target[None, :]) & valid_rows[None, :]
    ).astype(jnp.float32)
    dense_part = jnp.dot(
        placer, slot_sum, precision=lax.Precision.HIGHEST, preferred_element_type=jnp.float32
    )
    centroid_sums = lax.psum_scatter(dense_part, "fsdp", scatter_dimension=1, tiled=True)
    rows_dev = feat_dim // n_fsdp
    row_start = lax.axis_index("fsdp") * rows_dev
    shard_rows = lax.all_gather(residual, "fsdp", axis=0, tiled=True)
    left_cols = lax.dynamic_slice_in_dim(shard_rows, row_start, rows_dev, 1)
    gram_part = lax.dot_general(
        left_cols, shard_rows, (((0,), (0,)), ((), ())), preferred_element_type=jnp.float32
    )
    gram_sum = lax.psum_scatter(gram_part, "cent", scatter_dimension=1, tiled=True)
    tokens_all = tok_dev * n_fsdp * n_cent
    return (centroid_sums, gram_sum / tokens_all)


def solution(mesh):
    in_specs = (
        P("fsdp", "cent"),
        P("cent", "fsdp"),
        P(("fsdp", "cent"), None),
        P(),
        P("cent", None),
        P(("fsdp", "cent")),
        P("fsdp", None),
    )
    out_specs = (P("cent", "fsdp"), P("fsdp", "cent"))
    return jax.shard_map(shards, mesh=mesh, in_specs=in_specs, out_specs=out_specs, check_vma=False)
```

profile of v0, /device:TPU:1, one launch (start us, length us, event | category | flops | bytes accessed | tf_op | source)
XLA Modules:
  0.0 557.3 jit_solution(6380447563696765636)
XLA Ops:
  7.3 0.7 all-gather.4.cloned.1.call-update
  8.0 0.7 convert_bitcast_fusion
  8.7 0.2 reduce-window.8
  8.9 0.7 fusion.11
  9.5 0.1 select_reduce_fusion
  9.7 0.6 gather_fusion.1
  10.2 0.1 fusion.8
  10.4 0.7 select_select_fusion
  11.2 90.4 %all-gather.4.cloned.1.call-done = bf16[512,4096]{0,1:T(8,128)(2,1)} async-done(((bf16[512,64]{0,1:T(8,128)(2,1)}), bf16[512,4096]{0,1:T(8,128)(2,1)}) %all-gather.4.cloned.1.call-update) | async-done | bytes 4194320 | tf_op jit(solution)/shard_map/all_gather | solution.py:18
  101.6 4.8 convolution_convert_fusion
  106.4 0.0 all-reduce.2.cloned.1.call-start
  106.5 0.2 convert_reduce_fusion
  106.7 0.7 gather_fusion
  107.4 31.2 %all-gather.6.cloned.1.call-done = bf16[16,8,4096]{2,1,0:T(8,128)(2,1)} async-done(((bf16[2,8,4096]{2,1,0:T(8,128)(2,1)}), bf16[16,8,4096]{2,1,0:T(8,128)(2,1)}) %all-gather.6.cloned.1.call-update) | async-done | bytes 1048592 | tf_op jit(solution)/shard_map/all_gather | solution.py:51
  138.6 2.1 gather_fusion.2
  140.7 41.5 %reduce-scatter.6.cloned.1.call-done = bf16[16,4096]{1,0:T(8,128)(2,1)} async-done(((bf16[128,4096]{1,0:T(8,128)(2,1)}), bf16[16,4096]{1,0:T(8,128)(2,1)}) %reduce-scatter.6.cloned.1.call-update) | async-done | bytes 131088 | tf_op jit(solution)/shard_map/reduce_scatter | solution.py:21
  182.2 1.1 multiply_reduce_fusion
  183.2 1.0 subtract_convert_fusion
  184.3 1.1 convolution_convert_fusion.1
  185.5 0.5 all-gather.8.cloned.1.call-update
  186.1 0.1 iota_add_fusion
  186.1 0.1 add.94
  186.2 0.1 broadcast_in_dim.69
  186.3 0.1 and.75
  186.4 77.4 %all-reduce.2.cloned.1.call-done = bf16[64,4096]{1,0:T(8,128)(2,1)} async-done(((bf16[64,4096]{1,0:T(8,128)(2,1)}), bf16[64,4096]{1,0:T(8,128)(2,1)}) %all-reduce.2.cloned.1.call-update) | async-done | bytes 524304 | tf_op jit(solution)/shard_map/psum | solution.py:64
  263.8 2.9 convolution_bitcast_fusion
  266.8 91.8 %all-gather.8.cloned.1.call-done = bf16[1024,4096]{1,0:T(8,128)(2,1)} async-done(((bf16[16,4096]{1,0:T(8,128)(2,1)}), bf16[1024,4096]{1,0:T(8,128)(2,1)}) %all-gather.8.cloned.1.call-update) | async-done | bytes 8388624 | tf_op jit(solution)/shard_map/all_gather | solution.py:76
  358.6 6.1 %fusion = f32[64,4096]{1,0:T(8,128)} fusion(bf16[1024,4096]{1,0:T(8,128)(2,1)} %all-gather.8.cloned.1.call-done, s32[]{:T(128)S(6)} %select_n.78), kind=kOutput, calls=%fused_computation.6 | convolution fusion | flops 536870912 | bytes 9699332 | tf_op jit(solution)/shard_map/dot_general | solution.py:78
  364.8 139.4 %reduce-scatter.10.cloned.1.call-done = f32[64,64]{1,0:T(8,128)} async-done(((f32[4096,64]{1,0:T(8,128)}), f32[64,64]{1,0:T(8,128)}) %reduce-scatter.10.cloned.1.call-update) | async-done | bytes 16400
  504.1 1.5 copy.10
  505.6 43.3 %reduce-scatter.8.cloned.1.call-done = f32[64,512]{1,0:T(8,128)} async-done(((f32[64,4096]{1,0:T(8,128)}), f32[64,512]{1,0:T(8,128)}) %reduce-scatter.8.cloned.1.call-update) | async-done | bytes 131088 | tf_op jit(solution)/shard_map/reduce_scatter | solution.py:81
  548.9 1.6 broadcast_multiply_fusion
  (36 shorter events, 0.5 us)
Async XLA Ops:
  7.2 2.5 copy-start
  7.2 99.3 %copy-start.4 = (s32[1,8]{1,0:T(1,128)S(1)}, s32[1,8]{1,0:T(1,128)}, u32[]{:S(2)}) copy-start(s32[1,8]{1,0:T(1,128)} %param.13) | copy-start | bytes 100
  7.2 99.2 %copy-start.3 = (bf16[4096]{0:T(1024)(128)(2,1)S(1)}, bf16[4096]{0:T(1024)(128)(2,1)}, u32[]{:S(2)}) copy-start(bf16[4096]{0:T(1024)(128)(2,1)} %param.10) | copy-start | bytes 24580
  7.2 99.2 %copy-start.5 = (s32[16]{0:T(128)S(1)}, s32[16]{0:T(128)}, u32[]{:S(2)}) copy-start(s32[16]{0:T(128)} %param.12) | copy-start | bytes 196
  7.2 94.4 %all-gather.4.cloned.1.call-start = ((), (), s32[]{:S(2)}) async-start(), calls=%async_computation.3 | async-start | bytes 4259840 | tf_op jit(solution)/shard_map/all_gather | solution.py:18
  7.9 130.6 %all-gather.6.cloned.1.call-start = ((), (), s32[]{:S(2)}) async-start(), calls=%async_computation.5 | async-start | bytes 1179648 | tf_op jit(solution)/shard_map/all_gather | solution.py:51
  11.1 171.1 %copy-start.2 = (bf16[16,4096]{1,0:T(8,128)(2,1)S(1)}, bf16[16,4096]{1,0:T(8,128)(2,1)}, u32[]{:S(2)}) copy-start(bf16[16,4096]{1,0:T(8,128)(2,1)} %param.9) | copy-start | bytes 393220
  11.1 171.0 %reduce-scatter.6.cloned.1.call-start = ((), (), s32[]{:S(2)}) async-start(), calls=%async_computation.4 | async-start | bytes 1179648 | tf_op jit(solution)/shard_map/reduce_scatter | solution.py:21
  106.4 157.4 %all-reduce.2.cloned.1.call-start = ((), (), s32[]{:S(2)}) async-start(), calls=%async_computation.6 | async-start | bytes 1048576 | tf_op jit(solution)/shard_map/psum | solution.py:64
  184.3 1.2 copy-start.1
  185.4 173.2 %all-gather.8.cloned.1.call-start = ((), (), s32[]{:S(2)}) async-start(), calls=%async_computation.7 | async-start | bytes 8519680 | tf_op jit(solution)/shard_map/all_gather | solution.py:76
  186.0 318.1 %reduce-scatter.10.cloned.1.call-start = ((), (), s32[]{:S(2)}) async-start(), calls=%async_computation.9 | async-start | bytes 2129920
  266.7 282.2 %reduce-scatter.8.cloned.1.call-start = ((), (), s32[]{:S(2)}) async-start(), calls=%async_computation.8 | async-start | bytes 1179648 | tf_op jit(solution)/shard_map/reduce_scatter | solution.py:81
Sparse Core Ops, SparseCore 0:
  11.4 90.1 all-gather.3
  104.3 34.2 all-gather.5
  141.4 40.7 reduce-scatter.5
  185.5 78.1 all-reduce.1
  267.5 91.0 all-gather.7
  363.1 141.0 reduce-scatter.9
  507.0 41.8 reduce-scatter.7
where the time goes:
time: 561 us; the launch traced here: 557 us
  waiting for transfers between devices  516 us (92%)
  matrix products  14.9 us (3%)
  between operations  14.3 us (3%)
  other arithmetic  6.51 us (1%)
    unnamed x8, waiting for transfers between devices  141 us
    all_gather x1, waiting for transfers between devices, shards(): shard_rows = lax.all_gather(residual, 'fsdp', axis=0, tiled=True)  91.8 us
    all_gather x1, waiting for transfers between devices, shards(): lax.all_gather(w_out, 'fsdp', axis=1, tiled=True)  90.4 us
    psum x1, waiting for transfers between devices, shards(): lax.psum(slot_part.astype(jnp.bfloat16), 'cent').astype(jnp.float32)  77.4 us
    reduce_scatter x1, waiting for transfers between devices, shards(): lax.psum_scatter(gram_part, 'cent', scatter_dimension=1, tiled=True)  43.3 us
    reduce_scatter x1, waiting for transfers between devices, shards(): lax.psum_scatter(partial_out.astype(jnp.bfloat16), 'cent', scatter_dimens...  41.5 us
    all_gather x1, waiting for transfers between devices, shards(): arrived = lax.all_gather(outgoing, 'cent', axis=0, tiled=True)  31.2 us
  transfers between devices with their start and end apart: 7, of which 7 were waited for; matrix products, arithmetic and copies ran while one was open for 4% of the time, Pallas kernels for 0%

commit v1 on v0

v1 whole, which is shorter than its diff:
```python
import functools

import jax
import jax.numpy as jnp
from jax import lax
from jax.experimental import pallas as pl
from jax.experimental.pallas import tpu as pltpu
from jax.sharding import PartitionSpec as P

TILE = 8
LT = 8
MESH = pl.DeviceIdType.MESH


def swap_kernel(n, views, *refs):
    count = len(views)
    sources, landed = refs[:count], refs[count : 2 * count]
    send_sem, recv_sem, own_sem = refs[2 * count :]
    line = lax.axis_index("fsdp")
    me = lax.axis_index("cent")
    barrier = pltpu.get_barrier_semaphore()
    for step in range(1, n):
        pl.semaphore_signal(
            barrier, inc=1, device_id=(line, lax.rem(me + step, n)), device_id_type=MESH
        )
    pl.semaphore_wait(barrier, n - 1)
    copies = []
    for step in sorted(range(1, n), key=lambda s: -min(s, n - s)):
        peer = lax.rem(me + step, n)
        for which in range(count):
            copy = pltpu.make_async_remote_copy(
                src_ref=views[which](sources[which], peer),
                dst_ref=landed[which].at[me],
                send_sem=send_sem.at[which, step],
                recv_sem=recv_sem.at[which, step],
                device_id=(line, peer),
                device_id_type=MESH,
            )
            copy.start()
            copies.append(copy)
    owns = []
    for which in range(count):
        own = pltpu.make_async_copy(
            views[which](sources[which], me), landed[which].at[me], own_sem.at[which]
        )
        own.start()
        owns.append(own)
    for own in owns:
        own.wait()
    for copy in copies:
        copy.wait()


def swap(n, collective_id, operands, views, pieces, work_bytes):
    count = len(operands)
    return pl.pallas_call(
        functools.partial(swap_kernel, n, views),
        out_shape=[
            jax.ShapeDtypeStruct((n,) + piece, operand.dtype)
            for piece, operand in zip(pieces, operands)
        ],
        in_specs=[pl.BlockSpec(memory_space=pltpu.VMEM)] * count,
        out_specs=[pl.BlockSpec(memory_space=pltpu.VMEM)] * count,
        scratch_shapes=[
            pltpu.SemaphoreType.DMA((count, n)),
            pltpu.SemaphoreType.DMA((count, n)),
            pltpu.SemaphoreType.DMA((count,)),
        ],
        compiler_params=pltpu.CompilerParams(collective_id=collective_id, has_side_effects=True),
        cost_estimate=pl.CostEstimate(flops=0, bytes_accessed=work_bytes, transcendentals=0),
    )(*operands)


def whole(ref, peer):
    return ref


def row_piece(ref, peer):
    return ref.at[peer]


def shards(attention, w_out, hidden, norm_gain, centroids, token_codes, tile_lists):
    tok_dev = hidden.shape[0]
    feat_dim = hidden.shape[1]
    n_fsdp = lax.axis_size("fsdp")
    n_cent = lax.axis_size("cent")
    cap_slots = max(2, 2 * LT // n_cent)
    w_cols = lax.all_gather(w_out, "fsdp", axis=1, tiled=True)

    cent_dev = centroids.shape[0]
    own_tiles = cent_dev // TILE
    owner_idx = lax.axis_index("cent")
    listed = tile_lists[0]
    local_tile = listed - owner_idx * own_tiles
    owned_here = (local_tile >= 0) & (local_tile < own_tiles)
    safe_tile = jnp.clip(local_tile, 0, own_tiles - 1)
    tiles_here = centroids.reshape(own_tiles, TILE, feat_dim)
    slot_of = token_codes // TILE
    offset = token_codes % TILE
    list_pos = jnp.arange(LT, dtype=jnp.int32)
    owner_of = listed // own_tiles
    earlier = (owner_of[None, :] == owner_of[:, None]) & (list_pos[None, :] < list_pos[:, None])
    rank_all = jnp.sum(earlier.astype(jnp.int32), axis=1)
    chosen = owned_here[None, :] & (
        rank_all[None, :] == jnp.arange(cap_slots, dtype=jnp.int32)[:, None]
    )
    send_tile = jnp.sum(jnp.where(chosen, safe_tile[None, :], 0), axis=1)
    filled = jnp.any(chosen, axis=1)
    outgoing = jnp.where(
        filled[:, None, None],
        jnp.take(tiles_here, send_tile, axis=0),
        jnp.zeros((cap_slots, TILE, feat_dim), jnp.bfloat16),
    ).reshape(cap_slots * TILE, feat_dim)
    (arrived,) = swap(
        n_cent, 0, [outgoing], [whole], [(cap_slots * TILE, feat_dim)], 64 * 1024 * 1024
    )
    where_tile = owner_of * cap_slots + rank_all
    tile_rows = arrived.reshape(-1, feat_dim)
    centers = jnp.take(tile_rows, where_tile[slot_of] * TILE + offset, axis=0)
    tile_of = listed[slot_of]

    partial_out = jnp.dot(attention, w_cols, preferred_element_type=jnp.float32)
    (parts,) = swap(
        n_cent,
        1,
        [partial_out.astype(jnp.bfloat16).reshape(n_cent, tok_dev, feat_dim)],
        [row_piece],
        [(tok_dev, feat_dim)],
        64 * 1024 * 1024,
    )
    head_sum = jnp.sum(parts.astype(jnp.float32), axis=0)
    mixed_rows = hidden.astype(jnp.float32) + head_sum
    normed = (
        mixed_rows
        * lax.rsqrt(jnp.mean(mixed_rows * mixed_rows, axis=1, keepdims=True) + 1e-05)
        * norm_gain.astype(jnp.float32)
    )
    residual = (normed - centers.astype(jnp.float32)).astype(jnp.bfloat16)

    lane = jnp.arange(128, dtype=jnp.int32)[None, :]
    label = jnp.where(
        lane == 0, tile_of[:, None], jnp.where(lane == 1, offset[:, None], 0)
    ).astype(jnp.bfloat16)
    shard_rows = lax.all_gather(
        jnp.concatenate([residual, label], axis=1), "fsdp", axis=0, tiled=True
    )
    rows_dev = feat_dim // n_fsdp
    row_start = lax.axis_index("fsdp") * rows_dev
    left_cols = lax.dynamic_slice_in_dim(shard_rows, row_start, rows_dev, 1)
    gram_part = lax.dot_general(
        left_cols, shard_rows, (((0,), (0,)), ((), ())), preferred_element_type=jnp.float32
    ).astype(jnp.bfloat16)
    cent_id = (
        shard_rows[:, feat_dim].astype(jnp.float32) * TILE
        + shard_rows[:, feat_dim + 1].astype(jnp.float32)
    ).astype(jnp.int32)
    n_rows = cent_dev * n_cent
    onehot = (cent_id[None, :] == jnp.arange(n_rows, dtype=jnp.int32)[:, None]).astype(
        jnp.bfloat16
    )
    sums_part = jnp.dot(onehot, left_cols, preferred_element_type=jnp.float32)
    cols_dev = feat_dim // n_cent

    def col_piece(ref, peer):
        return ref.at[:, pl.ds(pl.multiple_of(peer * cols_dev, cols_dev), cols_dev)]

    gram_parts, sums_parts = swap(
        n_cent,
        2,
        [gram_part, sums_part.reshape(n_cent, cent_dev, rows_dev)],
        [col_piece, row_piece],
        [(rows_dev, cols_dev), (cent_dev, rows_dev)],
        64 * 1024 * 1024,
    )
    centroid_sums = jnp.sum(sums_parts, axis=0)
    gram_sum = jnp.sum(gram_parts.astype(jnp.float32), axis=0)
    tokens_all = tok_dev * n_fsdp * n_cent
    return (centroid_sums, gram_sum / tokens_all)


def solution(mesh):
    in_specs = (
        P("fsdp", "cent"),
        P("cent", "fsdp"),
        P(("fsdp", "cent"), None),
        P(),
        P("cent", None),
        P(("fsdp", "cent")),
        P("fsdp", None),
    )
    out_specs = (P("cent", "fsdp"), P("fsdp", "cent"))
    return jax.shard_map(shards, mesh=mesh, in_specs=in_specs, out_specs=out_specs, check_vma=False)
```

time: 561 us -> 272 us (0.48)
  waiting for transfers between devices: 516 us -> 130 us
  Pallas kernels: 0 us -> 96.3 us
  other arithmetic: 6.51 us -> 13 us
    unnamed x8 -> x2, waiting for transfers between devices: 141 us -> 0.7 us
    pallas_call x0 -> x3, Pallas kernels: none -> 96.3 us  [swap(): pl.pallas_call(functools.partial(swap_kernel, n, views), out_shape=[jax.S...]
    reduce_scatter x2 -> x0, waiting for transfers between devices: 84.7 us -> none  [the longest x1 43.3 us: shards(): lax.psum_scatter(gram_part, 'cent', scatter_dimension=1, tiled=True)]
    all_gather x3 -> x2, waiting for transfers between devices: 213 us -> 130 us  [the longest x1 83.4 us: shards(): lax.all_gather(jnp.concatenate([residual, label], axis=1), 'fsdp', axis=0...]
    psum x1 -> x0, waiting for transfers between devices: 77.4 us -> none  [shards(): lax.psum(slot_part.astype(jnp.bfloat16), 'cent').astype(jnp.float32)]
  transfers between devices with their start and end apart: 7 -> 2, of which waited for: 7 -> 2; matrix products, arithmetic and copies ran while one was open for 4% -> 4% of each run, Pallas kernels for 0% -> 13%
where the time goes in v1:
time: 272 us
  waiting for transfers between devices  130 us (48%)
  Pallas kernels  96.3 us (35%)
  between operations  14.2 us (5%)
  other arithmetic  13 us (5%)
  matrix products  12.9 us (5%)
  local copies, waits for them, and re-layouts  4.98 us (2%)
    pallas_call x3, Pallas kernels, swap(): pl.pallas_call(functools.partial(swap_kernel, n, views), out_shape=[jax.S...  96.3 us
    all_gather x1, waiting for transfers between devices, shards(): lax.all_gather(jnp.concatenate([residual, label], axis=1), 'fsdp', axis=0...  83.4 us
    all_gather x1, waiting for transfers between devices, shards(): w_cols = lax.all_gather(w_out, 'fsdp', axis=1, tiled=True)  46.2 us
    dot_general x1, matrix products, shards(): lax.dot_general(left_cols, shard_rows, (((0,), (0,)), ((), ())), preferre...  5.94 us
  transfers between devices with their start and end apart: 2, of which 2 were waited for; matrix products, arithmetic and copies ran while one was open for 4% of the time, Pallas kernels for 13%

profile of v1, /device:TPU:1, one launch (start us, length us, event | category | flops | bytes accessed | tf_op | source)
XLA Modules:
  0.0 271.7 jit_solution(15320141443686413061)
XLA Ops:
  7.2 0.7 all-gather.3.cloned.1.call-update
  8.0 0.7 and_select_fusion.3
  8.6 0.7 clamp_bitcast_fusion
  9.3 0.2 convert_reduce_fusion.3
  9.5 0.7 and_bitcast_fusion
  10.1 0.1 fusion.6
  10.4 0.1 select_reduce_fusion
  10.7 0.7 compare_select_fusion.3
  11.4 0.7 multiply_add_fusion
  12.1 0.7 gather_fusion
  12.7 1.3 gather_fusion.3
  14.0 0.7 convert_element_type.60
  14.8 0.6 gather_fusion.1
  15.3 0.7 fusion.4.refs_0_
  16.1 36.3 %shard_map.87 = bf16[8,16,4096]{2,1,0:T(8,128)(2,1)} custom-call(bf16[16,4096]{1,0:T(8,128)(2,1)} %fusion.4.refs_0_), custom_call_target="tpu_custom_call" | custom-call | bytes 67108864 | tf_op jit(solution)/shard_map/pallas_call | solution.py:56
  52.4 0.7 compare_and_fusion.2
  53.1 2.1 gather_fusion.2
  55.3 46.2 %all-gather.3.cloned.1.call-done = bf16[512,4096]{0,1:T(8,128)(2,1)} async-done(((bf16[512,64]{0,1:T(8,128)(2,1)}), bf16[512,4096]{0,1:T(8,128)(2,1)}) %all-gather.3.cloned.1.call-update) | async-done | bytes 4194320 | tf_op jit(solution)/shard_map/all_gather | solution.py:88
  101.5 4.7 %convolution_convert_fusion.1 = bf16[128,4096]{1,0:T(8,128)(2,1)} fusion(bf16[128,512]{1,0:T(8,128)(2,1)} %param.7, bf16[512,4096]{0,1:T(8,128)(2,1)} %all-gather.3.cloned.1.call-done), kind=kOutput, calls=%fused_computation.5 | convolution fusion | flops 537395200 | bytes 5373952 | tf_op jit(solution)/shard_map/dot_general | solution.py:122
  106.2 32.8 %shard_map.86 = bf16[8,16,4096]{2,1,0:T(8,128)(2,1)} custom-call(bf16[8,16,4096]{2,1,0:T(8,128)(2,1)} %bitcast.28), custom_call_target="tpu_custom_call" | custom-call | bytes 67108864 | tf_op jit(solution)/shard_map/pallas_call | solution.py:56
  139.0 1.4 convert_reduce_fusion
  140.4 0.2 multiply_reduce_fusion
  140.6 0.1 subtract_convert_fusion
  140.8 0.7 pad_maximum_fusion
  141.4 83.4 %all-gather.5.cloned.1.call-done = bf16[1024,4224]{1,0:T(8,128)(2,1)} async-done(((bf16[16,4224]{1,0:T(8,128)(2,1)}), bf16[1024,4224]{1,0:T(8,128)(2,1)}) %all-gather.5.cloned.1.call-update) | async-done | bytes 8650768 | tf_op jit(solution)/shard_map/all_gather | solution.py:144
  224.9 1.3 convert_reduce_fusion.2
  226.2 5.9 %convolution_convert_fusion.refs_0_ = bf16[64,4224]{1,0:T(8,128)(2,1)} fusion(bf16[1024,4224]{1,0:T(8,128)(2,1)} %all-gather.5.cloned.1.call-done, s32[]{:T(128)S(6)} %select_n.91), kind=kOutput, calls=%fused_computation.4 | convolution fusion | flops 553918464 | bytes 9453572 | tf_op jit(solution)/shard_map/dot_general | solution.py:150
  232.1 2.2 fusion
  234.3 27.1 %shard_map.88 = (bf16[8,64,512]{2,1,0:T(8,128)(2,1)}, f32[8,64,64]{2,1,0:T(8,128)}) custom-call(bf16[64,4224]{1,0:T(8,128)(2,1)} %convolution_convert_fusion.refs_0_, f32[8,64,64]{2,1,0:T(8,128)} %bitcast.29), custom_call_target="tpu_custom_call" | custom-call | bytes 67108864 | tf_op jit(solution)/shard_map/pallas_call | solution.py:56
  261.5 1.1 convert_reduce_fusion.1
  262.6 0.7 broadcast_multiply_fusion
  263.3 1.6 reduce_sum.61
  (19 shorter events, 0.6 us)
Async XLA Ops:
  7.2 7.6 %copy-start = (bf16[64,4096]{1,0:T(8,128)(2,1)S(1)}, bf16[64,4096]{1,0:T(8,128)(2,1)}, u32[]{:S(2)}) copy-start(bf16[64,4096]{1,0:T(8,128)(2,1)} %param.11) | copy-start | bytes 1572868
  7.2 94.3 %all-gather.3.cloned.1.call-start = ((), (), s32[]{:S(2)}) async-start(), calls=%async_computation | async-start | bytes 4259840 | tf_op jit(solution)/shard_map/all_gather | solution.py:88
  7.9 217.0 %all-gather.5.cloned.1.call-start = ((), (), s32[]{:S(2)}) async-start(), calls=%async_computation.1 | async-start | bytes 8785920 | tf_op jit(solution)/shard_map/all_gather | solution.py:144
  55.3 85.1 %copy-start.1 = (bf16[16,4096]{1,0:T(8,128)(2,1)S(1)}, bf16[16,4096]{1,0:T(8,128)(2,1)}, u32[]{:S(2)}) copy-start(bf16[16,4096]{1,0:T(8,128)(2,1)} %param.9) | copy-start | bytes 393220
Sparse Core Ops, SparseCore 0:
  11.3 90.1 all-gather.2
  141.6 83.2 all-gather.4

commit v2 on v1

--- a/solution.py
+++ b/solution.py
@@ -9,6 +9,8 @@
 
 TILE = 8
 LT = 8
+NY = 8
+NX = 4
 MESH = pl.DeviceIdType.MESH
 
 
@@ -71,8 +73,160 @@
     )(*operands)
 
 
-def whole(ref, peer):
-    return ref
+def ring_arrivals(size, sign):
+    arrivals = []
+    for hops in range(1, size // 2 + 1):
+        arrivals.append((hops, -sign * hops, sign, hops < size // 2))
+        if hops < size // 2:
+            arrivals.append((hops, sign * hops, -sign, hops < size // 2 - 1))
+    return arrivals
+
+
+def plane_kernel(n_cent, has_tiles, *refs):
+    if has_tiles:
+        block, tiles, out, tiles_out, send_sem, recv_sem, own_sem, tile_send, tile_recv, tile_own = refs
+    else:
+        block, out, send_sem, recv_sem, own_sem = refs
+    place = lax.axis_index("fsdp")
+    me = lax.axis_index("cent")
+    my_core = lax.rem(place, 2)
+    my_x = lax.rem(place // 2, NX)
+    my_y = place // (2 * NX)
+
+    def device_at(dy, dx, core):
+        return (lax.rem(my_y + dy + NY, NY) * NX + lax.rem(my_x + dx + NX, NX)) * 2 + core
+
+    barrier = pltpu.get_barrier_semaphore()
+    around = [device_at(dy, dx, my_core) for dy, dx in ((1, 0), (-1, 0), (0, 1), (0, -1))]
+    around.append(device_at(0, 0, 1 - my_core))
+    greeted = len(around)
+    for other in around:
+        pl.semaphore_signal(barrier, inc=1, device_id=(other, me), device_id_type=MESH)
+    if has_tiles:
+        greeted += n_cent - 1
+        for step in range(1, n_cent):
+            pl.semaphore_signal(
+                barrier, inc=1, device_id=(place, lax.rem(me + step, n_cent)), device_id_type=MESH
+            )
+    pl.semaphore_wait(barrier, greeted)
+
+    tile_copies = []
+    if has_tiles:
+        for step in sorted(range(1, n_cent), key=lambda s: -min(s, n_cent - s)):
+            copy = pltpu.make_async_remote_copy(
+                src_ref=tiles,
+                dst_ref=tiles_out.at[me],
+                send_sem=tile_send.at[step],
+                recv_sem=tile_recv.at[step],
+                device_id=(place, lax.rem(me + step, n_cent)),
+                device_id_type=MESH,
+            )
+            copy.start()
+            tile_copies.append(copy)
+
+    def walk(core, first_is_y, sign):
+        def offsets(first, second):
+            return (first, second) if first_is_y else (second, first)
+
+        sizes = (NY, NX) if first_is_y else (NX, NY)
+        copies = []
+
+        def send(source, origin, target):
+            copy = pltpu.make_async_remote_copy(
+                src_ref=source,
+                dst_ref=out.at[origin],
+                send_sem=send_sem.at[len(copies)],
+                recv_sem=recv_sem.at[origin],
+                device_id=(target, me),
+                device_id_type=MESH,
+            )
+            copy.start()
+            copies.append(copy)
+
+        def arrive(origin):
+            pltpu.make_async_remote_copy(
+                src_ref=out.at[origin],
+                dst_ref=out.at[origin],
+                send_sem=send_sem.at[0],
+                recv_sem=recv_sem.at[origin],
+                device_id=(device_at(0, 0, 1 - core), me),
+                device_id_type=MESH,
+            ).wait_recv()
+
+        firsts = [(0, 0, 0, False)] + ring_arrivals(sizes[0], sign)
+        seconds = ring_arrivals(sizes[1], sign)
+        events = []
+        for number, (hops, offset, way, goes_on) in enumerate(firsts):
+            events.append((hops, 0, number, 0, (offset, 0), way, goes_on))
+            for later, (more, across, turn, on_too) in enumerate(seconds):
+                events.append((hops + more, 1, number, later, (offset, across), turn, on_too))
+        for hops, leg, unused, also_unused, offset, way, goes_on in sorted(events):
+            origin = device_at(*offsets(*offset), core)
+            source = block
+            if hops > 0:
+                arrive(origin)
+                source = out.at[origin]
+            if leg == 0:
+                for turn in (1, -1) if hops == 0 else (way,) if goes_on else ():
+                    send(source, origin, device_at(*offsets(turn, 0), core))
+                for turn in (1, -1):
+                    send(source, origin, device_at(*offsets(0, turn), core))
+            elif goes_on:
+                send(source, origin, device_at(*offsets(0, way), core))
+            send(source, origin, device_at(0, 0, 1 - core))
+        own = pltpu.make_async_copy(block, out.at[place], own_sem)
+        own.start()
+        for chip in range(NY * NX):
+            arrive(2 * chip + 1 - core)
+        own.wait()
+        for copy in copies:
+            copy.wait_send()
+
+    @pl.when(my_core == 0)
+    def _():
+        walk(0, True, 1)
+
+    @pl.when(my_core == 1)
+    def _():
+        walk(1, False, -1)
+
+    if has_tiles:
+        own = pltpu.make_async_copy(tiles, tiles_out.at[me], tile_own)
+        own.start()
+        own.wait()
+        for copy in tile_copies:
+            copy.wait()
+
+
+def plane_gather(n_cent, collective_id, block, tiles=None):
+    devices = NY * NX * 2
+    operands = [block] if tiles is None else [block, tiles]
+    counts = [devices] if tiles is None else [devices, n_cent]
+    scratch = [
+        pltpu.SemaphoreType.DMA((devices,)),
+        pltpu.SemaphoreType.DMA((devices,)),
+        pltpu.SemaphoreType.DMA,
+    ]
+    if tiles is not None:
+        scratch += [
+            pltpu.SemaphoreType.DMA((n_cent,)),
+            pltpu.SemaphoreType.DMA((n_cent,)),
+            pltpu.SemaphoreType.DMA,
+        ]
+    return pl.pallas_call(
+        functools.partial(plane_kernel, n_cent, tiles is not None),
+        out_shape=[
+            jax.ShapeDtypeStruct((count,) + operand.shape, operand.dtype)
+            for count, operand in zip(counts, operands)
+        ],
+        in_specs=[pl.BlockSpec(memory_space=pltpu.VMEM)] * len(operands),
+        out_specs=[pl.BlockSpec(memory_space=pltpu.VMEM)] * len(operands),
+        scratch_shapes=scratch,
+        compiler_params=pltpu.CompilerParams(collective_id=collective_id, has_side_effects=True),
+        cost_estimate=pl.CostEstimate(
+            flops=0, bytes_accessed=64 * 1024 * 1024, transcendentals=0
+        ),
+    )(*operands)
 
 
 def row_piece(ref, peer):
@@ -85,8 +239,6 @@
     n_fsdp = lax.axis_size("fsdp")
     n_cent = lax.axis_size("cent")
     cap_slots = max(2, 2 * LT // n_cent)
-    w_cols = lax.all_gather(w_out, "fsdp", axis=1, tiled=True)
-
     cent_dev = centroids.shape[0]
     own_tiles = cent_dev // TILE
     owner_idx = lax.axis_index("cent")
@@ -111,15 +263,18 @@
         jnp.take(tiles_here, send_tile, axis=0),
         jnp.zeros((cap_slots, TILE, feat_dim), jnp.bfloat16),
     ).reshape(cap_slots * TILE, feat_dim)
-    (arrived,) = swap(
-        n_cent, 0, [outgoing], [whole], [(cap_slots * TILE, feat_dim)], 64 * 1024 * 1024
-    )
+    w_rows, arrived = plane_gather(n_cent, 0, w_out.T, outgoing)
     where_tile = owner_of * cap_slots + rank_all
     tile_rows = arrived.reshape(-1, feat_dim)
     centers = jnp.take(tile_rows, where_tile[slot_of] * TILE + offset, axis=0)
     tile_of = listed[slot_of]
 
-    partial_out = jnp.dot(attention, w_cols, preferred_element_type=jnp.float32)
+    partial_out = lax.dot_general(
+        attention,
+        w_rows.reshape(feat_dim, attention.shape[1]),
+        (((1,), (1,)), ((), ())),
+        preferred_element_type=jnp.float32,
+    )
     (parts,) = swap(
         n_cent,
         1,
@@ -141,9 +296,8 @@
     label = jnp.where(
         lane == 0, tile_of[:, None], jnp.where(lane == 1, offset[:, None], 0)
     ).astype(jnp.bfloat16)
-    shard_rows = lax.all_gather(
-        jnp.concatenate([residual, label], axis=1), "fsdp", axis=0, tiled=True
-    )
+    (gathered,) = plane_gather(n_cent, 3, jnp.concatenate([residual, label], axis=1))
+    shard_rows = gathered.reshape(-1, gathered.shape[-1])
     rows_dev = feat_dim // n_fsdp
     row_start = lax.axis_index("fsdp") * rows_dev
     left_cols = lax.dynamic_slice_in_dim(shard_rows, row_start, rows_dev, 1)

time: 272 us -> 176 us (0.65)
  waiting for transfers between devices: 130 us -> 0 us
  Pallas kernels: 96.3 us -> 144 us
  between operations: 14.2 us -> 0.78 us
    all_gather x2 -> x0, waiting for transfers between devices: 130 us -> none  [the longest x1 83.4 us: shards(): lax.all_gather(jnp.concatenate([residual, label], axis=1), 'fsdp', axis=0...]
    pallas_call x0 -> x2, Pallas kernels: none -> 88.3 us  [plane_gather(): pl.pallas_call(functools.partial(plane_kernel, n_cent, tiles is not None)...]
    pallas_call x3 -> x2, Pallas kernels: 96.3 us -> 55.3 us  [swap(): pl.pallas_call(functools.partial(swap_kernel, n, views), out_shape=[jax.S...]
  transfers between devices with their start and end apart: 2 -> 0, of which waited for: 2 -> 0; matrix products, arithmetic and copies ran while one was open for 4% -> 0% of each run, Pallas kernels for 13% -> 0%
where the time goes in v2:
time: 176 us; the launch traced here: 175 us
  Pallas kernels  144 us (82%)
  matrix products  12.9 us (7%)
  other arithmetic  11.7 us (7%)
  local copies, waits for them, and re-layouts  5.98 us (3%)
    pallas_call x2, Pallas kernels, plane_gather(): pl.pallas_call(functools.partial(plane_kernel, n_cent, tiles is not None)...  88.3 us
    pallas_call x2, Pallas kernels, swap(): pl.pallas_call(functools.partial(swap_kernel, n, views), out_shape=[jax.S...  55.3 us
    dot_general x1, matrix products, shards(): lax.dot_general(left_cols, shard_rows, (((0,), (0,)), ((), ())), preferre...  5.94 us
    dot_general x1, matrix products, shards(): lax.dot_general(attention, w_rows.reshape(feat_dim, attention.shape[1]),...  4.79 us

profile of v2, /device:TPU:1, one launch (start us, length us, event | category | flops | bytes accessed | tf_op | source)
XLA Modules:
  0.0 175.1 jit_solution(1559261347605675091)
XLA Ops:
  0.7 1.0 copy-done
  1.7 0.7 and_bitcast_fusion
  2.3 0.7 compare_select_fusion.1
  3.0 0.7 and_select_fusion.2
  3.7 0.7 clamp_bitcast_fusion
  4.3 0.2 convert_reduce_fusion.2
  4.5 0.1 select_reduce_fusion
  4.8 0.7 multiply_add_fusion
  5.8 0.7 gather_fusion.1
  6.4 1.3 gather_fusion.3
  7.8 0.7 compare_and_fusion
  8.5 0.7 convert_element_type.65
  9.2 0.6 gather_fusion
  9.8 0.7 fusion.4.refs_1_
  10.5 44.8 %shard_map.86 = (bf16[64,64,512]{2,1,0:T(8,128)(2,1)}, bf16[8,16,4096]{2,1,0:T(8,128)(2,1)}) custom-call(bf16[64,512]{1,0:T(8,128)(2,1)} %bitcast.40, bf16[16,4096]{1,0:T(8,128)(2,1)} %fusion.4.refs_1_), custom_call_target="tpu_custom_call" | custom-call | bytes 67108864 | tf_op jit(solution)/shard_map/pallas_call | solution.py:216
  55.4 4.8 %convolution_convert_fusion.1 = bf16[4096,128]{0,1:T(8,128)(2,1)} fusion(bf16[4096,512]{1,0:T(8,128)(2,1)} %bitcast.36, bf16[128,512]{1,0:T(8,128)(2,1)} %param.7), kind=kOutput, calls=%fused_computation.5 | convolution fusion | flops 537395200 | bytes 5373952 | tf_op jit(solution)/shard_map/dot_general | solution.py:272
  60.2 32.1 %shard_map.87 = bf16[8,16,4096]{2,1,0:T(8,128)(2,1)} custom-call(bf16[8,16,4096]{2,1,0:T(8,128)(2,1)} %bitcast.37), custom_call_target="tpu_custom_call" | custom-call | bytes 67108864 | tf_op jit(solution)/shard_map/pallas_call | solution.py:58
  92.3 1.4 convert_reduce_fusion
  93.7 0.6 gather_fusion.2
  94.3 0.2 multiply_reduce_fusion
  94.5 0.1 subtract_convert_fusion
  94.6 0.7 pad_maximum_fusion.refs_0_
  95.3 43.5 %shard_map.88 = bf16[64,16,4224]{2,1,0:T(8,128)(2,1)} custom-call(bf16[16,4224]{1,0:T(8,128)(2,1)} %pad_maximum_fusion.refs_0_), custom_call_target="tpu_custom_call" | custom-call | bytes 67108864 | tf_op jit(solution)/shard_map/pallas_call | solution.py:216
  138.8 1.2 fusion.11
  140.0 0.1 copy.17
  140.1 0.1 copy.18
  140.3 2.2 %fusion = f32[512,64]{1,0:T(8,128)} fusion(s32[1024]{0:T(1024)S(1)} %bitcast.41, bf16[1024,4224]{1,0:T(8,128)(2,1)} %bitcast.34, s32[]{:T(128)S(6)} %select_n.91), kind=kOutput, calls=%fused_computation.8 | convolution fusion | flops 67633152 | bytes 397316 | tf_op jit(solution)/shard_map/dot_general | solution.py:315
  142.5 5.9 %convolution_convert_fusion.refs_0_ = bf16[64,4224]{1,0:T(8,128)(2,1)} fusion(bf16[1024,4224]{1,0:T(8,128)(2,1)} %bitcast.35, s32[]{:T(128)S(6)} %select_n.91), kind=kOutput, calls=%fused_computation.4 | convolution fusion | flops 553918464 | bytes 9453572 | tf_op jit(solution)/shard_map/dot_general | solution.py:304
  148.4 23.3 %shard_map.89 = (bf16[8,64,512]{2,1,0:T(8,128)(2,1)}, f32[8,64,64]{2,1,0:T(8,128)}) custom-call(bf16[64,4224]{1,0:T(8,128)(2,1)} %convolution_convert_fusion.refs_0_, f32[8,64,64]{2,1,0:T(8,128)} %bitcast.39), custom_call_target="tpu_custom_call" | custom-call | bytes 67108864 | tf_op jit(solution)/shard_map/pallas_call | solution.py:58
  171.7 1.6 reduce_sum.61
  173.3 1.1 convert_reduce_fusion.1
  174.4 0.7 broadcast_multiply_fusion
  (19 shorter events, 0.6 us)
Async XLA Ops:
  0.6 1.0 copy-start
  55.4 38.3 %copy-start.1 = (bf16[8,16,4096]{2,1,0:T(8,128)(2,1)S(1)}, bf16[8,16,4096]{2,1,0:T(8,128)(2,1)}, u32[]{:S(2)}) copy-start(bf16[8,16,4096]{2,1,0:T(8,128)(2,1)} %get-tuple-element.7) | copy-start | bytes 3145732
  55.4 38.9 %copy-start.2 = (bf16[16,4096]{1,0:T(8,128)(2,1)S(1)}, bf16[16,4096]{1,0:T(8,128)(2,1)}, u32[]{:S(2)}) copy-start(bf16[16,4096]{1,0:T(8,128)(2,1)} %param.9) | copy-start | bytes 393220

commit v3 on v2

--- a/solution.py
+++ b/solution.py
@@ -17,29 +17,71 @@
 def swap_kernel(n, views, *refs):
     count = len(views)
     sources, landed = refs[:count], refs[count : 2 * count]
-    send_sem, recv_sem, own_sem = refs[2 * count :]
+    send_sem, recv_sem, own_sem, hop_send, hop_recv = refs[2 * count : 2 * count + 5]
+    relay = refs[2 * count + 5 :]
     line = lax.axis_index("fsdp")
     me = lax.axis_index("cent")
+    my_core = lax.rem(line, 2)
+    far, mid = n // 2, n // 4
     barrier = pltpu.get_barrier_semaphore()
     for step in range(1, n):
         pl.semaphore_signal(
             barrier, inc=1, device_id=(line, lax.rem(me + step, n)), device_id_type=MESH
         )
     pl.semaphore_wait(barrier, n - 1)
-    copies = []
-    for step in sorted(range(1, n), key=lambda s: -min(s, n - s)):
+
+    def remote(source, target, sent, got, peer):
+        return pltpu.make_async_remote_copy(
+            src_ref=source,
+            dst_ref=target,
+            send_sem=sent,
+            recv_sem=got,
+            device_id=(line, peer),
+            device_id_type=MESH,
+        )
+
+    def direct(which, step):
         peer = lax.rem(me + step, n)
-        for which in range(count):
-            copy = pltpu.make_async_remote_copy(
-                src_ref=views[which](sources[which], peer),
-                dst_ref=landed[which].at[me],
-                send_sem=send_sem.at[which, step],
-                recv_sem=recv_sem.at[which, step],
-                device_id=(line, peer),
-                device_id_type=MESH,
-            )
-            copy.start()
-            copies.append(copy)
+        return remote(
+            views[which](sources[which], peer),
+            landed[which].at[me],
+            send_sem.at[which, step],
+            recv_sem.at[which, step],
+            peer,
+        )
+
+    def first_hop(which):
+        return remote(
+            views[which](sources[which], lax.rem(me + far, n)),
+            relay[which],
+            hop_send.at[which],
+            hop_recv.at[which],
+            lax.rem(me + n - mid, n),
+        )
+
+    def second_hop(which):
+        return remote(
+            relay[which],
+            landed[which].at[lax.rem(me + mid, n)],
+            send_sem.at[which, far],
+            recv_sem.at[which, far],
+            lax.rem(me + n - mid, n),
+        )
+
+    @pl.when(my_core == 0)
+    def _():
+        for which in range(count):
+            direct(which, far).start()
+
+    @pl.when(my_core == 1)
+    def _():
+        for which in range(count):
+            first_hop(which).start()
+
+    near = sorted((s for s in range(1, n) if s != far), key=lambda s: -min(s, n - s))
+    for step in near:
+        for which in range(count):
+            direct(which, step).start()
     owns = []
     for which in range(count):
         own = pltpu.make_async_copy(
@@ -47,10 +89,28 @@
         )
         own.start()
         owns.append(own)
+
+    @pl.when(my_core == 1)
+    def _():
+        for which in range(count):
+            first_hop(which).wait()
+            second_hop(which).start()
+
     for own in owns:
         own.wait()
-    for copy in copies:
-        copy.wait()
+    for step in near:
+        for which in range(count):
+            direct(which, step).wait()
+
+    @pl.when(my_core == 0)
+    def _():
+        for which in range(count):
+            direct(which, far).wait()
+
+    @pl.when(my_core == 1)
+    def _():
+        for which in range(count):
+            second_hop(which).wait()
 
 
 def swap(n, collective_id, operands, views, pieces, work_bytes):
@@ -67,7 +127,10 @@
             pltpu.SemaphoreType.DMA((count, n)),
             pltpu.SemaphoreType.DMA((count, n)),
             pltpu.SemaphoreType.DMA((count,)),
-        ],
+            pltpu.SemaphoreType.DMA((count,)),
+            pltpu.SemaphoreType.DMA((count,)),
+        ]
+        + [pltpu.VMEM(piece, operand.dtype) for piece, operand in zip(pieces, operands)],
         compiler_params=pltpu.CompilerParams(collective_id=collective_id, has_side_effects=True),
         cost_estimate=pl.CostEstimate(flops=0, bytes_accessed=work_bytes, transcendentals=0),
     )(*operands)
@@ -257,12 +320,7 @@
         rank_all[None, :] == jnp.arange(cap_slots, dtype=jnp.int32)[:, None]
     )
     send_tile = jnp.sum(jnp.where(chosen, safe_tile[None, :], 0), axis=1)
-    filled = jnp.any(chosen, axis=1)
-    outgoing = jnp.where(
-        filled[:, None, None],
-        jnp.take(tiles_here, send_tile, axis=0),
-        jnp.zeros((cap_slots, TILE, feat_dim), jnp.bfloat16),
-    ).reshape(cap_slots * TILE, feat_dim)
+    outgoing = jnp.take(tiles_here, send_tile, axis=0).reshape(cap_slots * TILE, feat_dim)
     w_rows, arrived = plane_gather(n_cent, 0, w_out.T, outgoing)
     where_tile = owner_of * cap_slots + rank_all
     tile_rows = arrived.reshape(-1, feat_dim)
@@ -312,7 +370,7 @@
     onehot = (cent_id[None, :] == jnp.arange(n_rows, dtype=jnp.int32)[:, None]).astype(
         jnp.bfloat16
     )
-    sums_part = jnp.dot(onehot, left_cols, preferred_element_type=jnp.float32)
+    sums_part = jnp.dot(onehot, left_cols, preferred_element_type=jnp.float32).astype(jnp.bfloat16)
     cols_dev = feat_dim // n_cent
 
     def col_piece(ref, peer):
@@ -326,7 +384,7 @@
         [(rows_dev, cols_dev), (cent_dev, rows_dev)],
         64 * 1024 * 1024,
     )
-    centroid_sums = jnp.sum(sums_parts, axis=0)
+    centroid_sums = jnp.sum(sums_parts.astype(jnp.float32), axis=0)
     gram_sum = jnp.sum(gram_parts.astype(jnp.float32), axis=0)
     tokens_all = tok_dev * n_fsdp * n_cent
     return (centroid_sums, gram_sum / tokens_all)

time: 176 us -> 176 us (level)
  no operation moved by 1% of the time
where the time goes in v3:
time: 176 us
  Pallas kernels  145 us (82%)
  matrix products  12.2 us (7%)
  other arithmetic  11.5 us (7%)
  local copies, waits for them, and re-layouts  6.58 us (4%)
    pallas_call x2, Pallas kernels, plane_gather(): pl.pallas_call(functools.partial(plane_kernel, n_cent, tiles is not None)...  88.2 us
    pallas_call x2, Pallas kernels, swap(): pl.pallas_call(functools.partial(swap_kernel, n, views), out_shape=[jax.S...  56.4 us
    dot_general x1, matrix products, shards(): lax.dot_general(left_cols, shard_rows, (((0,), (0,)), ((), ())), preferre...  5.94 us
    dot_general x1, matrix products, shards(): lax.dot_general(attention, w_rows.reshape(feat_dim, attention.shape[1]),...  4.78 us

profile of v3, /device:TPU:1, one launch (start us, length us, event | category | flops | bytes accessed | tf_op | source)
XLA Modules:
  0.0 175.7 jit_solution(15485725865796980462)
XLA Ops:
  0.7 1.0 copy-done
  1.7 0.7 compare_select_fusion.1
  2.3 0.7 and_bitcast_fusion
  3.0 0.7 and_select_fusion.3
  3.7 0.7 clamp_bitcast_fusion
  4.3 0.2 convert_reduce_fusion.3
  4.6 0.7 multiply_add_fusion
  5.5 0.7 gather_fusion.1
  6.2 1.3 gather_fusion.3
  7.5 0.7 compare_and_fusion
  8.3 0.7 convert_element_type.71
  9.0 0.6 gather_fusion
  9.5 0.7 bitcast_select_fusion.refs_1_
  10.3 44.8 %shard_map.86 = (bf16[64,64,512]{2,1,0:T(8,128)(2,1)}, bf16[8,16,4096]{2,1,0:T(8,128)(2,1)}) custom-call(bf16[64,512]{1,0:T(8,128)(2,1)} %bitcast.38, bf16[16,4096]{1,0:T(8,128)(2,1)} %bitcast_select_fusion.refs_1_), custom_call_target="tpu_custom_call" | custom-call | bytes 67108864 | tf_op jit(solution)/shard_map/pallas_call | solution.py:279
  55.1 4.8 %convolution_convert_fusion.1 = bf16[4096,128]{0,1:T(8,128)(2,1)} fusion(bf16[4096,512]{1,0:T(8,128)(2,1)} %bitcast.34, bf16[128,512]{1,0:T(8,128)(2,1)} %param.7), kind=kOutput, calls=%fused_computation.5 | convolution fusion | flops 537395200 | bytes 5373952 | tf_op jit(solution)/shard_map/dot_general | solution.py:330
  59.9 32.6 %shard_map.87 = bf16[8,16,4096]{2,1,0:T(8,128)(2,1)} custom-call(bf16[8,16,4096]{2,1,0:T(8,128)(2,1)} %bitcast.35), custom_call_target="tpu_custom_call" | custom-call | bytes 67108864 | tf_op jit(solution)/shard_map/pallas_call | solution.py:118
  92.5 1.4 convert_reduce_fusion
  93.9 0.6 gather_fusion.2
  94.5 0.2 multiply_reduce_fusion
  94.7 0.1 subtract_convert_fusion
  94.8 0.7 pad_maximum_fusion.refs_0_
  95.5 43.4 %shard_map.88 = bf16[64,16,4224]{2,1,0:T(8,128)(2,1)} custom-call(bf16[16,4224]{1,0:T(8,128)(2,1)} %pad_maximum_fusion.refs_0_), custom_call_target="tpu_custom_call" | custom-call | bytes 67108864 | tf_op jit(solution)/shard_map/pallas_call | solution.py:279
  138.8 1.2 fusion.11
  140.0 0.1 copy.16
  140.2 0.1 copy.17
  140.3 1.5 fusion.1
  141.9 5.9 %convolution_convert_fusion.refs_0_ = bf16[64,4224]{1,0:T(8,128)(2,1)} fusion(bf16[1024,4224]{1,0:T(8,128)(2,1)} %bitcast.33, s32[]{:T(128)S(6)} %select_n.85), kind=kOutput, calls=%fused_computation.4 | convolution fusion | flops 553918464 | bytes 9453572 | tf_op jit(solution)/shard_map/dot_general | solution.py:362
  147.8 0.8 copy.15
  148.6 23.8 %shard_map.89 = (bf16[8,64,512]{2,1,0:T(8,128)(2,1)}, bf16[8,64,64]{2,1,0:T(8,128)(2,1)}) custom-call(bf16[64,4224]{1,0:T(8,128)(2,1)} %convolution_convert_fusion.refs_0_, bf16[8,64,64]{2,1,0:T(8,128)(2,1)} %bitcast.37), custom_call_target="tpu_custom_call" | custom-call | bytes 67108864 | tf_op jit(solution)/shard_map/pallas_call | solution.py:118
  172.4 1.6 convert_reduce_fusion.2
  173.9 1.1 convert_reduce_fusion.1
  175.0 0.7 broadcast_multiply_fusion
  (17 shorter events, 0.4 us)
Async XLA Ops:
  0.6 1.0 copy-start
  55.1 38.8 %copy-start.1 = (bf16[8,16,4096]{2,1,0:T(8,128)(2,1)S(1)}, bf16[8,16,4096]{2,1,0:T(8,128)(2,1)}, u32[]{:S(2)}) copy-start(bf16[8,16,4096]{2,1,0:T(8,128)(2,1)} %get-tuple-element.7) | copy-start | bytes 3145732
  55.1 39.4 %copy-start.2 = (bf16[16,4096]{1,0:T(8,128)(2,1)S(1)}, bf16[16,4096]{1,0:T(8,128)(2,1)}, u32[]{:S(2)}) copy-start(bf16[16,4096]{1,0:T(8,128)(2,1)} %param.9) | copy-start | bytes 393220

commit v4 on v1

--- a/solution.py
+++ b/solution.py
@@ -9,35 +9,79 @@
 
 TILE = 8
 LT = 8
+NY = 8
+NX = 4
 MESH = pl.DeviceIdType.MESH
 
 
 def swap_kernel(n, views, *refs):
     count = len(views)
     sources, landed = refs[:count], refs[count : 2 * count]
-    send_sem, recv_sem, own_sem = refs[2 * count :]
+    send_sem, recv_sem, own_sem, hop_send, hop_recv = refs[2 * count : 2 * count + 5]
+    relay = refs[2 * count + 5 :]
     line = lax.axis_index("fsdp")
     me = lax.axis_index("cent")
+    my_core = lax.rem(line, 2)
+    far, mid = n // 2, n // 4
     barrier = pltpu.get_barrier_semaphore()
     for step in range(1, n):
         pl.semaphore_signal(
             barrier, inc=1, device_id=(line, lax.rem(me + step, n)), device_id_type=MESH
         )
     pl.semaphore_wait(barrier, n - 1)
-    copies = []
-    for step in sorted(range(1, n), key=lambda s: -min(s, n - s)):
+
+    def remote(source, target, sent, got, peer):
+        return pltpu.make_async_remote_copy(
+            src_ref=source,
+            dst_ref=target,
+            send_sem=sent,
+            recv_sem=got,
+            device_id=(line, peer),
+            device_id_type=MESH,
+        )
+
+    def direct(which, step):
         peer = lax.rem(me + step, n)
-        for which in range(count):
-            copy = pltpu.make_async_remote_copy(
-                src_ref=views[which](sources[which], peer),
-                dst_ref=landed[which].at[me],
-                send_sem=send_sem.at[which, step],
-                recv_sem=recv_sem.at[which, step],
-                device_id=(line, peer),
-                device_id_type=MESH,
-            )
-            copy.start()
-            copies.append(copy)
+        return remote(
+            views[which](sources[which], peer),
+            landed[which].at[me],
+            send_sem.at[which, step],
+            recv_sem.at[which, step],
+            peer,
+        )
+
+    def first_hop(which):
+        return remote(
+            views[which](sources[which], lax.rem(me + far, n)),
+            relay[which],
+            hop_send.at[which],
+            hop_recv.at[which],
+            lax.rem(me + n - mid, n),
+        )
+
+    def second_hop(which):
+        return remote(
+            relay[which],
+            landed[which].at[lax.rem(me + mid, n)],
+            send_sem.at[which, far],
+            recv_sem.at[which, far],
+            lax.rem(me + n - mid, n),
+        )
+
+    @pl.when(my_core == 0)
+    def _():
+        for which in range(count):
+            direct(which, far).start()
+
+    @pl.when(my_core == 1)
+    def _():
+        for which in range(count):
+            first_hop(which).start()
+
+    near = sorted((s for s in range(1, n) if s != far), key=lambda s: -min(s, n - s))
+    for step in near:
+        for which in range(count):
+            direct(which, step).start()
     owns = []
     for which in range(count):
         own = pltpu.make_async_copy(
@@ -45,10 +89,28 @@
         )
         own.start()
         owns.append(own)
+
+    @pl.when(my_core == 1)
+    def _():
+        for which in range(count):
+            first_hop(which).wait()
+            second_hop(which).start()
+
     for own in owns:
         own.wait()
-    for copy in copies:
-        copy.wait()
+    for step in near:
+        for which in range(count):
+            direct(which, step).wait()
+
+    @pl.when(my_core == 0)
+    def _():
+        for which in range(count):
+            direct(which, far).wait()
+
+    @pl.when(my_core == 1)
+    def _():
+        for which in range(count):
+            second_hop(which).wait()
 
 
 def swap(n, collective_id, operands, views, pieces, work_bytes):
@@ -65,14 +127,284 @@
             pltpu.SemaphoreType.DMA((count, n)),
             pltpu.SemaphoreType.DMA((count, n)),
             pltpu.SemaphoreType.DMA((count,)),
-        ],
+            pltpu.SemaphoreType.DMA((count,)),
+            pltpu.SemaphoreType.DMA((count,)),
+        ]
+        + [pltpu.VMEM(piece, operand.dtype) for piece, operand in zip(pieces, operands)],
         compiler_params=pltpu.CompilerParams(collective_id=collective_id, has_side_effects=True),
         cost_estimate=pl.CostEstimate(flops=0, bytes_accessed=work_bytes, transcendentals=0),
     )(*operands)
 
 
-def whole(ref, peer):
-    return ref
+def ring_arrivals(size, sign):
+    arrivals = []
+    for hops in range(1, size // 2 + 1):
+        arrivals.append((hops, -sign * hops, sign, hops < size // 2))
+        if hops < size // 2:
+            arrivals.append((hops, sign * hops, -sign, hops < size // 2 - 1))
+    return arrivals
+
+
+def chip_order():
+    def hops(chip):
+        return min(chip[0], NY - chip[0]) + min(chip[1], NX - chip[1])
+
+    return sorted(((dy, dx) for dy in range(NY) for dx in range(NX)), key=lambda c: (hops(c), c))
+
+
+def plane_device(place, dy, dx, core):
+    x = lax.rem(place // 2, NX)
+    y = place // (2 * NX)
+    return (lax.rem(y + dy + NY, NY) * NX + lax.rem(x + dx + NX, NX)) * 2 + core
+
+
+def greet(place, me, peers):
+    my_core = lax.rem(place, 2)
+    barrier = pltpu.get_barrier_semaphore()
+    around = [plane_device(place, dy, dx, my_core) for dy, dx in ((1, 0), (-1, 0), (0, 1), (0, -1))]
+    around.append(plane_device(place, 0, 0, 1 - my_core))
+    for other in around:
+        pl.semaphore_signal(barrier, inc=1, device_id=(other, me), device_id_type=MESH)
+    for peer in peers:
+        pl.semaphore_signal(barrier, inc=1, device_id=(place, peer), device_id_type=MESH)
+    pl.semaphore_wait(barrier, len(around) + len(peers))
+
+
+def plane_walk(core, place, me, block, out, send_sem, recv_sem, own_sem, after=None):
+    first_is_y, sign = core == 0, 1 - 2 * core
+
+    def offsets(first, second):
+        return (first, second) if first_is_y else (second, first)
+
+    def device_at(dy, dx, which):
+        return plane_device(place, dy, dx, which)
+
+    sizes = (NY, NX) if first_is_y else (NX, NY)
+    copies = []
+    here = {(0, 0, core)}
+
+    def send(source, origin, target):
+        copy = pltpu.make_async_remote_copy(
+            src_ref=source,
+            dst_ref=out.at[origin],
+            send_sem=send_sem.at[len(copies)],
+            recv_sem=recv_sem.at[origin],
+            device_id=(target, me),
+            device_id_type=MESH,
+        )
+        copy.start()
+        copies.append(copy)
+
+    def arrive(dy, dx, which):
+        if (dy % NY, dx % NX, which) in here:
+            return
+        here.add((dy % NY, dx % NX, which))
+        origin = device_at(dy, dx, which)
+        pltpu.make_async_remote_copy(
+            src_ref=out.at[origin],
+            dst_ref=out.at[origin],
+            send_sem=send_sem.at[0],
+            recv_sem=recv_sem.at[origin],
+            device_id=(device_at(0, 0, 1 - core), me),
+            device_id_type=MESH,
+        ).wait_recv()
+
+    own = pltpu.make_async_copy(block, out.at[place], own_sem)
+    own.start()
+    firsts = [(0, 0, 0, False)] + ring_arrivals(sizes[0], sign)
+    seconds = ring_arrivals(sizes[1], sign)
+    events = []
+    for number, (hops, offset, way, goes_on) in enumerate(firsts):
+        events.append((hops, 0, number, 0, (offset, 0), way, goes_on))
+        for later, (more, across, turn, on_too) in enumerate(seconds):
+            events.append((hops + more, 1, number, later, (offset, across), turn, on_too))
+    events.sort()
+    for at, (hops, leg, unused, also_unused, offset, way, goes_on) in enumerate(events):
+        dy, dx = offsets(*offset)
+        origin = device_at(dy, dx, core)
+        source = block
+        if hops > 0:
+            arrive(dy, dx, core)
+            source = out.at[origin]
+        if leg == 0:
+            for turn in (1, -1) if hops == 0 else (way,) if goes_on else ():
+                send(source, origin, device_at(*offsets(turn, 0), core))
+            for turn in (1, -1):
+                send(source, origin, device_at(*offsets(0, turn), core))
+        elif goes_on:
+            send(source, origin, device_at(*offsets(0, way), core))
+        send(source, origin, device_at(0, 0, 1 - core))
+        if at + 1 == len(events) or events[at + 1][0] > hops:
+            if hops == 0:
+                own.wait()
+            if after is not None:
+                after(hops, arrive)
+    for dy, dx in chip_order():
+        arrive(dy, dx, 1 - core)
+    for copy in copies:
+        copy.wait_send()
+
+
+def plane_kernel(block, out, send_sem, recv_sem, own_sem):
+    place, me = lax.axis_index("fsdp"), lax.axis_index("cent")
+    greet(place, me, [])
+    for core in range(2):
+
+        @pl.when(lax.rem(place, 2) == core)
+        def _():
+            plane_walk(core, place, me, block, out, send_sem, recv_sem, own_sem)
+
+
+def plane_gather(collective_id, block):
+    devices = NY * NX * 2
+    return pl.pallas_call(
+        plane_kernel,
+        out_shape=jax.ShapeDtypeStruct((devices,) + block.shape, block.dtype),
+        in_specs=[pl.BlockSpec(memory_space=pltpu.VMEM)],
+        out_specs=pl.BlockSpec(memory_space=pltpu.VMEM),
+        scratch_shapes=[
+            pltpu.SemaphoreType.DMA((devices,)),
+            pltpu.SemaphoreType.DMA((devices,)),
+            pltpu.SemaphoreType.DMA,
+        ],
+        compiler_params=pltpu.CompilerParams(collective_id=collective_id, has_side_effects=True),
+    )(block)
+
+
+GROUPS = 4
+
+
+def project_kernel(n, *refs):
+    attention, block, tiles, head, tiles_out = refs[:5]
+    w_all, stage, landed, send_sem, recv_sem, own_sem, part_send, part_recv = refs[5:13]
+    tile_send, tile_recv, tile_own = refs[13:]
+    place, me = lax.axis_index("fsdp"), lax.axis_index("cent")
+    greet(place, me, [lax.rem(me + step, n) for step in range(1, n)])
+    order = chip_order()
+    per_group = len(order) // GROUPS
+    tok_dev = head.shape[0]
+
+    def part(group, step):
+        peer = lax.rem(me + step, n)
+        slots = pl.ds(group * per_group, per_group)
+        return pltpu.make_async_remote_copy(
+            src_ref=stage.at[peer, slots],
+            dst_ref=landed.at[step, slots],
+            send_sem=part_send.at[group, step],
+            recv_sem=part_recv.at[group, step],
+            device_id=(place, peer),
+            device_id_type=MESH,
+        )
+
+    def tile(source, origin, offset, way):
+        return pltpu.make_async_remote_copy(
+            src_ref=source,
+            dst_ref=tiles_out.at[origin],
+            send_sem=tile_send.at[(offset - way) % n],
+            recv_sem=tile_recv.at[(offset - way) % n],
+            device_id=(place, lax.rem(me + way + n, n)),
+            device_id_type=MESH,
+        )
+
+    def run(core):
+        turns = ring_arrivals(n, 1 - 2 * core) if n > 2 else [(1, 1, -1, False)]
+        sent = []
+
+        def pass_tiles(hops):
+            if hops == 0:
+                for way in (1, -1) if n > 2 else (1,):
+                    copy = tile(tiles, me, 0, way)
+                    copy.start()
+                    sent.append(copy)
+            for steps, offset, way, goes_on in turns:
+                if steps == hops:
+                    origin = lax.rem(me + offset + n, n)
+                    tile(tiles_out.at[origin], origin, offset + way, way).wait_recv()
+                    if goes_on:
+                        copy = tile(tiles_out.at[origin], origin, offset, way)
+                        copy.start()
+                        sent.append(copy)
+
+        def multiply(group, arrive):
+            rows = attention[...]
+            for slot in range(group * per_group, (group + 1) * per_group):
+                dy, dx = order[slot]
+                arrive(dy, dx, 0)
+                arrive(dy, dx, 1)
+                both = w_all[pl.ds(plane_device(place, dy, dx, 0), 2)]
+                columns = lax.dot_general(
+                    rows,
+                    both.reshape(2 * both.shape[1], both.shape[2]),
+                    (((1,), (1,)), ((), ())),
+                    preferred_element_type=jnp.float32,
+                ).astype(jnp.bfloat16)
+                stage[:, slot] = columns.reshape(n, tok_dev, columns.shape[1])
+            for step in sorted(range(1, n), key=lambda s: -min(s, n - s)):
+                part(group, step).start()
+
+        def after(hops, arrive):
+            pass_tiles(hops)
+            if 3 <= hops <= 5:
+                multiply(hops - 3, arrive)
+            elif hops == 6:
+                multiply(3, arrive)
+
+        plane_walk(core, place, me, block, w_all, send_sem, recv_sem, own_sem, after)
+        for copy in sent:
+            copy.wait_send()
+
+    for core in range(2):
+
+        @pl.when(lax.rem(place, 2) == core)
+        def _():
+            run(core)
+
+    own = pltpu.make_async_copy(tiles, tiles_out.at[me], tile_own)
+    own.start()
+    for group in range(GROUPS):
+        for step in range(1, n):
+            part(group, step).wait()
+        for slot in range(group * per_group, (group + 1) * per_group):
+            total = stage[me, slot].astype(jnp.float32)
+            for step in range(1, n):
+                total = total + landed[step, slot].astype(jnp.float32)
+            dy, dx = order[slot]
+            start = pl.multiple_of(plane_device(place, dy, dx, 0) // 2 * 128, 128)
+            head[:, pl.ds(start, 128)] = total
+    own.wait()
+
+
+def project(n, collective_id, attention, block, tiles):
+    devices = NY * NX * 2
+    tok_dev = attention.shape[0] // n
+    chips = NY * NX
+    wide = 2 * block.shape[0]
+    pieces = pltpu.VMEM((n, chips, tok_dev, wide), jnp.bfloat16)
+    return pl.pallas_call(
+        functools.partial(project_kernel, n),
+        out_shape=[
+            jax.ShapeDtypeStruct((tok_dev, chips * wide), jnp.float32),
+            jax.ShapeDtypeStruct((n,) + tiles.shape, tiles.dtype),
+        ],
+        in_specs=[pl.BlockSpec(memory_space=pltpu.VMEM)] * 3,
+        out_specs=[pl.BlockSpec(memory_space=pltpu.VMEM)] * 2,
+        scratch_shapes=[
+            pltpu.VMEM((devices,) + block.shape, block.dtype),
+            pieces,
+            pieces,
+            pltpu.SemaphoreType.DMA((devices,)),
+            pltpu.SemaphoreType.DMA((devices,)),
+            pltpu.SemaphoreType.DMA,
+            pltpu.SemaphoreType.DMA((GROUPS, n)),
+            pltpu.SemaphoreType.DMA((GROUPS, n)),
+            pltpu.SemaphoreType.DMA((n,)),
+            pltpu.SemaphoreType.DMA((n,)),
+            pltpu.SemaphoreType.DMA,
+        ],
+        compiler_params=pltpu.CompilerParams(
+            collective_id=collective_id, has_side_effects=True, vmem_limit_bytes=32 * 1024 * 1024
+        ),
+    )(attention, block, tiles)
 
 
 def row_piece(ref, peer):
@@ -85,8 +417,6 @@
     n_fsdp = lax.axis_size("fsdp")
     n_cent = lax.axis_size("cent")
     cap_slots = max(2, 2 * LT // n_cent)
-    w_cols = lax.all_gather(w_out, "fsdp", axis=1, tiled=True)
-
     cent_dev = centroids.shape[0]
     own_tiles = cent_dev // TILE
     owner_idx = lax.axis_index("cent")
@@ -105,30 +435,13 @@
         rank_all[None, :] == jnp.arange(cap_slots, dtype=jnp.int32)[:, None]
     )
     send_tile = jnp.sum(jnp.where(chosen, safe_tile[None, :], 0), axis=1)
-    filled = jnp.any(chosen, axis=1)
-    outgoing = jnp.where(
-        filled[:, None, None],
-        jnp.take(tiles_here, send_tile, axis=0),
-        jnp.zeros((cap_slots, TILE, feat_dim), jnp.bfloat16),
-    ).reshape(cap_slots * TILE, feat_dim)
-    (arrived,) = swap(
-        n_cent, 0, [outgoing], [whole], [(cap_slots * TILE, feat_dim)], 64 * 1024 * 1024
-    )
+    outgoing = jnp.take(tiles_here, send_tile, axis=0).reshape(cap_slots * TILE, feat_dim)
+    head_sum, arrived = project(n_cent, 0, attention, w_out.T, outgoing)
     where_tile = owner_of * cap_slots + rank_all
     tile_rows = arrived.reshape(-1, feat_dim)
     centers = jnp.take(tile_rows, where_tile[slot_of] * TILE + offset, axis=0)
     tile_of = listed[slot_of]
 
-    partial_out = jnp.dot(attention, w_cols, preferred_element_type=jnp.float32)
-    (parts,) = swap(
-        n_cent,
-        1,
-        [partial_out.astype(jnp.bfloat16).reshape(n_cent, tok_dev, feat_dim)],
-        [row_piece],
-        [(tok_dev, feat_dim)],
-        64 * 1024 * 1024,
-    )
-    head_sum = jnp.sum(parts.astype(jnp.float32), axis=0)
     mixed_rows = hidden.astype(jnp.float32) + head_sum
     normed = (
         mixed_rows
@@ -141,9 +454,8 @@
     label = jnp.where(
         lane == 0, tile_of[:, None], jnp.where(lane == 1, offset[:, None], 0)
     ).astype(jnp.bfloat16)
-    shard_rows = lax.all_gather(
-        jnp.concatenate([residual, label], axis=1), "fsdp", axis=0, tiled=True
-    )
+    gathered = plane_gather(3, jnp.concatenate([residual, label], axis=1))
+    shard_rows = gathered.reshape(-1, gathered.shape[-1])
     rows_dev = feat_dim // n_fsdp
     row_start = lax.axis_index("fsdp") * rows_dev
     left_cols = lax.dynamic_slice_in_dim(shard_rows, row_start, rows_dev, 1)
@@ -158,7 +470,7 @@
     onehot = (cent_id[None, :] == jnp.arange(n_rows, dtype=jnp.int32)[:, None]).astype(
         jnp.bfloat16
     )
-    sums_part = jnp.dot(onehot, left_cols, preferred_element_type=jnp.float32)
+    sums_part = jnp.dot(onehot, left_cols, preferred_element_type=jnp.float32).astype(jnp.bfloat16)
     cols_dev = feat_dim // n_cent
 
     def col_piece(ref, peer):
@@ -172,7 +484,7 @@
         [(rows_dev, cols_dev), (cent_dev, rows_dev)],
         64 * 1024 * 1024,
     )
-    centroid_sums = jnp.sum(sums_parts, axis=0)
+    centroid_sums = jnp.sum(sums_parts.astype(jnp.float32), axis=0)
     gram_sum = jnp.sum(gram_parts.astype(jnp.float32), axis=0)
     tokens_all = tok_dev * n_fsdp * n_cent
     return (centroid_sums, gram_sum / tokens_all)

time: 272 us -> 153 us (0.56)
  waiting for transfers between devices: 130 us -> 0 us
  Pallas kernels: 96.3 us -> 125 us
  between operations: 14.2 us -> 0.75 us
  matrix products: 12.9 us -> 7.46 us
  local copies, waits for them, and re-layouts: 4.98 us -> 8.3 us
    all_gather x2 -> x0, waiting for transfers between devices: 130 us -> none  [the longest x1 83.4 us: shards(): lax.all_gather(jnp.concatenate([residual, label], axis=1), 'fsdp', axis=0...]
    pallas_call x0 -> x2, Pallas kernels: none -> 100 us  [the longest x1 54 us: project(): pl.pallas_call(functools.partial(project_kernel, n), out_shape=[jax.Shape...]
    pallas_call x3 -> x1, Pallas kernels: 96.3 us -> 24.5 us  [swap(): pl.pallas_call(functools.partial(swap_kernel, n, views), out_shape=[jax.S...]
    dot_general x2 -> x1, matrix products: 6.91 us -> 1.51 us  [shards(): jnp.dot(onehot, left_cols, preferred_element_type=jnp.float32)]
    unnamed x4 -> x8, local copies, waits for them, and re-layouts: 0.01 us -> 3.05 us
  transfers between devices with their start and end apart: 2 -> 0, of which waited for: 2 -> 0; matrix products, arithmetic and copies ran while one was open for 4% -> 0% of each run, Pallas kernels for 13% -> 0%
where the time goes in v4:
time: 153 us
  Pallas kernels  125 us (82%)
  other arithmetic  11.3 us (7%)
  local copies, waits for them, and re-layouts  8.3 us (5%)
  matrix products  7.46 us (5%)
    pallas_call x1, Pallas kernels, project(): pl.pallas_call(functools.partial(project_kernel, n), out_shape=[jax.Shape...  54 us
    pallas_call x1, Pallas kernels, plane_gather(): pl.pallas_call(plane_kernel, out_shape=jax.ShapeDtypeStruct((devices,) +...  46.3 us
    pallas_call x1, Pallas kernels, swap(): pl.pallas_call(functools.partial(swap_kernel, n, views), out_shape=[jax.S...  24.5 us
    dot_general x1, matrix products, shards(): lax.dot_general(left_cols, shard_rows, (((0,), (0,)), ((), ())), preferre...  5.94 us

profile of v4, /device:TPU:1, one launch (start us, length us, event | category | flops | bytes accessed | tf_op | source)
XLA Modules:
  0.0 152.7 jit_solution(8130951680771471026)
XLA Ops:
  0.7 1.0 copy-done
  1.7 0.7 compare_select_fusion.1
  2.3 0.7 and_bitcast_fusion
  3.0 0.7 and_select_fusion.3
  3.7 0.7 clamp_bitcast_fusion
  4.3 0.2 convert_reduce_fusion.2
  4.5 0.1 fusion.6
  4.6 0.7 multiply_add_fusion
  5.4 0.1 broadcast_in_dim.97
  5.5 0.7 gather_fusion.1
  6.2 1.3 gather_fusion.3
  7.5 0.7 compare_and_fusion
  8.3 0.7 convert_element_type.59
  9.0 0.6 gather_fusion
  9.6 0.9 copy-done.1
  10.5 0.8 copy-done.2
  11.4 54.0 %shard_map.86 = (f32[16,4096]{1,0:T(8,128)S(1)}, bf16[8,16,4096]{2,1,0:T(8,128)(2,1)S(1)}) custom-call(bf16[128,512]{1,0:T(8,128)(2,1)S(1)} %copy-done.1, bf16[64,512]{1,0:T(8,128)(2,1)S(1)} %bitcast.25, bf16[16,4096]{1,0:T(8,128)(2,1)S(1)} %bitcast_select_fusion.refs_2_), custom_call_target="tpu_custom_call" | custom-call | tf_op jit(solution)/shard_map/pallas_call | solution.py:383
  65.4 0.6 gather_fusion.2
  66.0 1.1 multiply_reduce_fusion
  67.1 1.0 subtract_convert_fusion
  68.1 0.7 pad_maximum_fusion.block
  68.8 46.3 %shard_map.87 = bf16[64,16,4224]{2,1,0:T(8,128)(2,1)} custom-call(bf16[16,4224]{1,0:T(8,128)(2,1)} %pad_maximum_fusion.block), custom_call_target="tpu_custom_call" | custom-call | tf_op jit(solution)/shard_map/pallas_call | solution.py:260
  115.1 1.2 fusion.11
  116.2 0.1 copy.16
  116.4 0.1 copy.17
  116.5 1.5 fusion.1
  118.1 5.9 %convolution_convert_fusion.refs_0_ = bf16[64,4224]{1,0:T(8,128)(2,1)} fusion(bf16[1024,4224]{1,0:T(8,128)(2,1)} %bitcast.29, s32[]{:T(128)S(6)} %select_n.85), kind=kOutput, calls=%fused_computation.4 | convolution fusion | flops 553918464 | bytes 9453572 | tf_op jit(solution)/shard_map/dot_general | solution.py:462
  124.0 0.8 copy.15
  124.8 24.5 %shard_map.88 = (bf16[8,64,512]{2,1,0:T(8,128)(2,1)}, bf16[8,64,64]{2,1,0:T(8,128)(2,1)}) custom-call(bf16[64,4224]{1,0:T(8,128)(2,1)} %convolution_convert_fusion.refs_0_, bf16[8,64,64]{2,1,0:T(8,128)(2,1)} %bitcast.30), custom_call_target="tpu_custom_call" | custom-call | bytes 67108864 | tf_op jit(solution)/shard_map/pallas_call | solution.py:118
  149.3 1.6 %convert_reduce_fusion.1 = f32[64,64]{1,0:T(8,128)} fusion(bf16[8,64,64]{2,1,0:T(8,128)(2,1)} %get-tuple-element.8), kind=kLoop, calls=%fused_computation.10 | loop fusion | flops 61440 | bytes 81920 | tf_op jit(solution)/shard_map/reduce_sum | solution.py:487
  150.9 1.1 convert_reduce_fusion
  152.0 0.7 broadcast_multiply_fusion
  (14 shorter events, 0.3 us)
Async XLA Ops:
  0.6 1.0 copy-start
  9.6 0.9 copy-start.1
  10.5 0.8 copy-start.2

commit v5 on v4

--- a/solution.py
+++ b/solution.py
@@ -12,128 +12,6 @@
 NY = 8
 NX = 4
 MESH = pl.DeviceIdType.MESH
-
-
-def swap_kernel(n, views, *refs):
-    count = len(views)
-    sources, landed = refs[:count], refs[count : 2 * count]
-    send_sem, recv_sem, own_sem, hop_send, hop_recv = refs[2 * count : 2 * count + 5]
-    relay = refs[2 * count + 5 :]
-    line = lax.axis_index("fsdp")
-    me = lax.axis_index("cent")
-    my_core = lax.rem(line, 2)
-    far, mid = n // 2, n // 4
-    barrier = pltpu.get_barrier_semaphore()
-    for step in range(1, n):
-        pl.semaphore_signal(
-            barrier, inc=1, device_id=(line, lax.rem(me + step, n)), device_id_type=MESH
-        )
-    pl.semaphore_wait(barrier, n - 1)
-
-    def remote(source, target, sent, got, peer):
-        return pltpu.make_async_remote_copy(
-            src_ref=source,
-            dst_ref=target,
-            send_sem=sent,
-            recv_sem=got,
-            device_id=(line, peer),
-            device_id_type=MESH,
-        )
-
-    def direct(which, step):
-        peer = lax.rem(me + step, n)
-        return remote(
-            views[which](sources[which], peer),
-            landed[which].at[me],
-            send_sem.at[which, step],
-            recv_sem.at[which, step],
-            peer,
-        )
-
-    def first_hop(which):
-        return remote(
-            views[which](sources[which], lax.rem(me + far, n)),
-            relay[which],
-            hop_send.at[which],
-            hop_recv.at[which],
-            lax.rem(me + n - mid, n),
-        )
-
-    def second_hop(which):
-        return remote(
-            relay[which],
-            landed[which].at[lax.rem(me + mid, n)],
-            send_sem.at[which, far],
-            recv_sem.at[which, far],
-            lax.rem(me + n - mid, n),
-        )
-
-    @pl.when(my_core == 0)
-    def _():
-        for which in range(count):
-            direct(which, far).start()
-
-    @pl.when(my_core == 1)
-    def _():
-        for which in range(count):
-            first_hop(which).start()
-
-    near = sorted((s for s in range(1, n) if s != far), key=lambda s: -min(s, n - s))
-    for step in near:
-        for which in range(count):
-            direct(which, step).start()
-    owns = []
-    for which in range(count):
-        own = pltpu.make_async_copy(
-            views[which](sources[which], me), landed[which].at[me], own_sem.at[which]
-        )
-        own.start()
-        owns.append(own)
-
-    @pl.when(my_core == 1)
-    def _():
-        for which in range(count):
-            first_hop(which).wait()
-            second_hop(which).start()
-
-    for own in owns:
-        own.wait()
-    for step in near:
-        for which in range(count):
-            direct(which, step).wait()
-
-    @pl.when(my_core == 0)
-    def _():
-        for which in range(count):
-            direct(which, far).wait()
-
-    @pl.when(my_core == 1)
-    def _():
-        for which in range(count):
-            second_hop(which).wait()
-
-
-def swap(n, collective_id, operands, views, pieces, work_bytes):
-    count = len(operands)
-    return pl.pallas_call(
-        functools.partial(swap_kernel, n, views),
-        out_shape=[
-            jax.ShapeDtypeStruct((n,) + piece, operand.dtype)
-            for piece, operand in zip(pieces, operands)
-        ],
-        in_specs=[pl.BlockSpec(memory_space=pltpu.VMEM)] * count,
-        out_specs=[pl.BlockSpec(memory_space=pltpu.VMEM)] * count,
-        scratch_shapes=[
-            pltpu.SemaphoreType.DMA((count, n)),
-            pltpu.SemaphoreType.DMA((count, n)),
-            pltpu.SemaphoreType.DMA((count,)),
-            pltpu.SemaphoreType.DMA((count,)),
-            pltpu.SemaphoreType.DMA((count,)),
-        ]
-        + [pltpu.VMEM(piece, operand.dtype) for piece, operand in zip(pieces, operands)],
-        compiler_params=pltpu.CompilerParams(collective_id=collective_id, has_side_effects=True),
-        cost_estimate=pl.CostEstimate(flops=0, bytes_accessed=work_bytes, transcendentals=0),
-    )(*operands)
 
 
 def ring_arrivals(size, sign):
@@ -245,32 +123,6 @@
         copy.wait_send()
 
 
-def plane_kernel(block, out, send_sem, recv_sem, own_sem):
-    place, me = lax.axis_index("fsdp"), lax.axis_index("cent")
-    greet(place, me, [])
-    for core in range(2):
-
-        @pl.when(lax.rem(place, 2) == core)
-        def _():
-            plane_walk(core, place, me, block, out, send_sem, recv_sem, own_sem)
-
-
-def plane_gather(collective_id, block):
-    devices = NY * NX * 2
-    return pl.pallas_call(
-        plane_kernel,
-        out_shape=jax.ShapeDtypeStruct((devices,) + block.shape, block.dtype),
-        in_specs=[pl.BlockSpec(memory_space=pltpu.VMEM)],
-        out_specs=pl.BlockSpec(memory_space=pltpu.VMEM),
-        scratch_shapes=[
-            pltpu.SemaphoreType.DMA((devices,)),
-            pltpu.SemaphoreType.DMA((devices,)),
-            pltpu.SemaphoreType.DMA,
-        ],
-        compiler_params=pltpu.CompilerParams(collective_id=collective_id, has_side_effects=True),
-    )(block)
-
-
 GROUPS = 4
 
 
@@ -407,14 +259,111 @@
     )(attention, block, tiles)
 
 
-def row_piece(ref, peer):
-    return ref.at[peer]
+def moments_kernel(n, tokens, *refs):
+    block, sums, gram, rows, gram_out, gram_in, sums_out, sums_in = refs[:8]
+    send_sem, recv_sem, own_sem, gram_send, gram_recv, sums_send, sums_recv = refs[8:]
+    place, me = lax.axis_index("fsdp"), lax.axis_index("cent")
+    greet(place, me, [lax.rem(me + step, n) for step in range(1, n)])
+    rows_dev, cols_dev = gram.shape
+    cent_dev = sums.shape[0]
+    feat_dim = n * cols_dev
+    count = rows.shape[0] * rows.shape[1]
+    far_first = sorted(range(1, n), key=lambda s: -min(s, n - s))
+
+    def part(step, source, target, sent, got):
+        peer = lax.rem(me + step, n)
+        return pltpu.make_async_remote_copy(
+            src_ref=source.at[peer],
+            dst_ref=target.at[step],
+            send_sem=sent.at[step],
+            recv_sem=got.at[step],
+            device_id=(place, peer),
+            device_id_type=MESH,
+        )
+
+    def gram_part(step):
+        return part(step, gram_out, gram_in, gram_send, gram_recv)
+
+    def sums_part(step):
+        return part(step, sums_out, sums_in, sums_send, sums_recv)
+
+    def run(core):
+        plane_walk(core, place, me, block, rows, send_sem, recv_sem, own_sem)
+        pair = rows[:, :, pl.ds(pl.multiple_of(place // 2 * 128, 128), 128)].reshape(count, 128)
+        half = slice(rows_dev * core, rows_dev * (core + 1))
+        left = pair.T[half]
+        for step in far_first + [0]:
+            peer = lax.rem(me + step, n)
+            right = rows[:, :, pl.ds(pl.multiple_of(peer * cols_dev, cols_dev), cols_dev)]
+            gram_out[peer] = jnp.dot(
+                left, right.reshape(count, cols_dev), preferred_element_type=jnp.float32
+            ).astype(jnp.bfloat16)
+            if step > 0:
+                gram_part(step).start()
+        label = rows[:, :, feat_dim:].reshape(count, 128).T[:8].astype(jnp.float32)
+        cent_id = label[0:1] * TILE + label[1:2]
+        number = lax.broadcasted_iota(jnp.int32, (n * cent_dev, count), 0).astype(jnp.float32)
+        onehot = jnp.where(number == cent_id, 1.0, 0.0).astype(jnp.bfloat16)
+        both = jnp.dot(onehot, pair, preferred_element_type=jnp.float32)
+        sums_out[...] = both[:, half].astype(jnp.bfloat16).reshape(n, cent_dev, rows_dev)
+        for step in far_first:
+            sums_part(step).start()
+
+    for core in range(2):
+
+        @pl.when(lax.rem(place, 2) == core)
+        def _():
+            run(core)
+
+    total = gram_out[me].astype(jnp.float32)
+    for step in range(1, n):
+        gram_part(step).wait()
+        total = total + gram_in[step].astype(jnp.float32)
+    gram[...] = total * (1.0 / tokens)
+    total = sums_out[me].astype(jnp.float32)
+    for step in range(1, n):
+        sums_part(step).wait()
+        total = total + sums_in[step].astype(jnp.float32)
+    sums[...] = total
+
+
+def moments(n, collective_id, block, feat_dim, cent_dev):
+    devices = NY * NX * 2
+    rows_dev, cols_dev = feat_dim // devices, feat_dim // n
+    tokens = block.shape[0] * devices * n
+    gram_pieces = pltpu.VMEM((n, rows_dev, cols_dev), jnp.bfloat16)
+    sums_pieces = pltpu.VMEM((n, cent_dev, rows_dev), jnp.bfloat16)
+    return pl.pallas_call(
+        functools.partial(moments_kernel, n, tokens),
+        out_shape=[
+            jax.ShapeDtypeStruct((cent_dev, rows_dev), jnp.float32),
+            jax.ShapeDtypeStruct((rows_dev, cols_dev), jnp.float32),
+        ],
+        in_specs=[pl.BlockSpec(memory_space=pltpu.VMEM)],
+        out_specs=[pl.BlockSpec(memory_space=pltpu.VMEM)] * 2,
+        scratch_shapes=[
+            pltpu.VMEM((devices,) + block.shape, block.dtype),
+            gram_pieces,
+            gram_pieces,
+            sums_pieces,
+            sums_pieces,
+            pltpu.SemaphoreType.DMA((devices,)),
+            pltpu.SemaphoreType.DMA((devices,)),
+            pltpu.SemaphoreType.DMA,
+            pltpu.SemaphoreType.DMA((n,)),
+            pltpu.SemaphoreType.DMA((n,)),
+            pltpu.SemaphoreType.DMA((n,)),
+            pltpu.SemaphoreType.DMA((n,)),
+        ],
+        compiler_params=pltpu.CompilerParams(
+            collective_id=collective_id, has_side_effects=True, vmem_limit_bytes=48 * 1024 * 1024
+        ),
+    )(block)
 
 
 def shards(attention, w_out, hidden, norm_gain, centroids, token_codes, tile_lists):
     tok_dev = hidden.shape[0]
     feat_dim = hidden.shape[1]
-    n_fsdp = lax.axis_size("fsdp")
     n_cent = lax.axis_size("cent")
     cap_slots = max(2, 2 * LT // n_cent)
     cent_dev = centroids.shape[0]
@@ -454,40 +403,9 @@
     label = jnp.where(
         lane == 0, tile_of[:, None], jnp.where(lane == 1, offset[:, None], 0)
     ).astype(jnp.bfloat16)
-    gathered = plane_gather(3, jnp.concatenate([residual, label], axis=1))
-    shard_rows = gathered.reshape(-1, gathered.shape[-1])
-    rows_dev = feat_dim // n_fsdp
-    row_start = lax.axis_index("fsdp") * rows_dev
-    left_cols = lax.dynamic_slice_in_dim(shard_rows, row_start, rows_dev, 1)
-    gram_part = lax.dot_general(
-        left_cols, shard_rows, (((0,), (0,)), ((), ())), preferred_element_type=jnp.float32
-    ).astype(jnp.bfloat16)
-    cent_id = (
-        shard_rows[:, feat_dim].astype(jnp.float32) * TILE
-        + shard_rows[:, feat_dim + 1].astype(jnp.float32)
-    ).astype(jnp.int32)
-    n_rows = cent_dev * n_cent
-    onehot = (cent_id[None, :] == jnp.arange(n_rows, dtype=jnp.int32)[:, None]).astype(
-        jnp.bfloat16
+    return tuple(
+        moments(n_cent, 1, jnp.concatenate([residual, label], axis=1), feat_dim, cent_dev)
     )
-    sums_part = jnp.dot(onehot, left_cols, preferred_element_type=jnp.float32).astype(jnp.bfloat16)
-    cols_dev = feat_dim // n_cent
-
-    def col_piece(ref, peer):
-        return ref.at[:, pl.ds(pl.multiple_of(peer * cols_dev, cols_dev), cols_dev)]
-
-    gram_parts, sums_parts = swap(
-        n_cent,
-        2,
-        [gram_part, sums_part.reshape(n_cent, cent_dev, rows_dev)],
-        [col_piece, row_piece],
-        [(rows_dev, cols_dev), (cent_dev, rows_dev)],
-        64 * 1024 * 1024,
-    )
-    centroid_sums = jnp.sum(sums_parts.astype(jnp.float32), axis=0)
-    gram_sum = jnp.sum(gram_parts.astype(jnp.float32), axis=0)
-    tokens_all = tok_dev * n_fsdp * n_cent
-    return (centroid_sums, gram_sum / tokens_all)
 
 
 def solution(mesh):

time: 153 us -> 123 us (0.80)
  other arithmetic: 11.3 us -> 0.87 us
  Pallas kernels: 125 us -> 115 us
  matrix products: 7.46 us -> 0 us
  local copies, waits for them, and re-layouts: 8.3 us -> 6.37 us
    pallas_call x2 -> x1, Pallas kernels: 70.8 us -> 61.2 us  [moments(): pl.pallas_call(functools.partial(moments_kernel, n, tokens), out_shape=[j...]
    dot_general x2 -> x0, matrix products: 7.46 us -> none  [the longest x1 5.94 us: shards(): lax.dot_general(left_cols, shard_rows, (((0,), (0,)), ((), ())), preferre...]
    reduce_sum x2 -> x0, other arithmetic: 2.68 us -> none  [the longest x1 1.55 us: shards(): centroid_sums = jnp.sum(sums_parts.astype(jnp.float32), axis=0)]
    unnamed x8 -> x16, local copies, waits for them, and re-layouts: 3.05 us -> 3.72 us
where the time goes in v5:
time: 123 us
  Pallas kernels  115 us (93%)
  local copies, waits for them, and re-layouts  6.37 us (5%)
    pallas_call x1, Pallas kernels, moments(): pl.pallas_call(functools.partial(moments_kernel, n, tokens), out_shape=[j...  61.2 us
    pallas_call x1, Pallas kernels, project(): pl.pallas_call(functools.partial(project_kernel, n), out_shape=[jax.Shape...  54 us
    unnamed x16, local copies, waits for them, and re-layouts  3.72 us

profile of v5, /device:TPU:1, one launch (start us, length us, event | category | flops | bytes accessed | tf_op | source)
XLA Modules:
  0.0 123.2 jit_solution(8245947171246515954)
XLA Ops:
  0.6 0.0 copy-start
  0.6 0.0 copy-start.3
  0.7 0.7 copy-done.3
  1.4 0.2 convert_reduce_fusion
  1.6 0.0 copy-start.6
  1.6 0.6 copy-done.6
  2.3 0.7 gather_fusion.1
  2.9 0.7 gather_fusion.3
  3.6 0.1 select_convert_fusion
  3.7 0.0 copy-done
  3.7 0.1 fusion.1
  3.8 0.6 gather_fusion
  4.4 0.1 broadcast_in_dim.94
  4.5 0.1 broadcast_in_dim.95
  4.6 0.0 copy-start.1
  4.6 0.0 copy-start.2
  4.6 0.1 bitcast_select_fusion.refs_2_
  4.7 0.8 copy-done.1
  5.5 0.0 copy-done.2
  5.5 54.0 %shard_map.86 = (f32[16,4096]{1,0:T(8,128)S(1)}, bf16[8,16,4096]{2,1,0:T(8,128)(2,1)S(1)}) custom-call(bf16[128,512]{1,0:T(8,128)(2,1)S(1)} %copy-done.1, bf16[64,512]{1,0:T(8,128)(2,1)S(1)} %bitcast.21, bf16[16,4096]{1,0:T(8,128)(2,1)S(1)} %bitcast_select_fusion.refs_2_), custom_call_target="tpu_custom_call" | custom-call | tf_op jit(solution)/shard_map/pallas_call | solution.py:235
  59.5 0.0 copy-start.5
  59.5 0.0 copy-start.4
  59.5 0.6 gather_fusion.2
  60.1 0.0 copy-done.5
  60.2 0.2 copy-done.4
  60.4 0.2 multiply_reduce_fusion
  60.6 0.1 subtract_convert_fusion
  60.7 61.2 %shard_map.87 = (f32[64,64]{1,0:T(8,128)S(1)}, f32[64,512]{1,0:T(8,128)S(1)}) custom-call(bf16[16,4224]{1,0:T(8,128)(2,1)S(1)} %pad_maximum_fusion.refs_0_), custom_call_target="tpu_custom_call" | custom-call | tf_op jit(solution)/shard_map/pallas_call | solution.py:336
  122.0 0.6 copy.11
  122.6 0.7 copy.12
  (15 shorter events, 0.1 us)
Async XLA Ops:
  0.6 3.1 %copy-start = (bf16[64,4096]{1,0:T(8,128)(2,1)S(1)}, bf16[64,4096]{1,0:T(8,128)(2,1)}, u32[]{:S(2)}) copy-start(bf16[64,4096]{1,0:T(8,128)(2,1)} %param.11) | copy-start | bytes 1572868
  0.6 0.7 copy-start.3
  1.6 0.7 copy-start.6
  4.6 0.9 copy-start.1
  4.6 0.9 copy-start.2
  59.5 0.7 copy-start.5
  59.5 0.9 copy-start.4

commit v6 on v5

--- a/solution.py
+++ b/solution.py
@@ -196,8 +196,8 @@
 
         def after(hops, arrive):
             pass_tiles(hops)
-            if 3 <= hops <= 5:
-                multiply(hops - 3, arrive)
+            if 2 <= hops <= 4:
+                multiply(hops - 2, arrive)
             elif hops == 6:
                 multiply(3, arrive)
 

time: 123 us -> 122 us (level)
    pallas_call x1, Pallas kernels: 61.2 us -> 59.5 us  [moments(): pl.pallas_call(functools.partial(moments_kernel, n, tokens), out_shape=[j...]
where the time goes in v6:
time: 122 us
  Pallas kernels  114 us (93%)
  local copies, waits for them, and re-layouts  6.37 us (5%)
    pallas_call x1, Pallas kernels, moments(): pl.pallas_call(functools.partial(moments_kernel, n, tokens), out_shape=[j...  59.5 us
    pallas_call x1, Pallas kernels, project(): pl.pallas_call(functools.partial(project_kernel, n), out_shape=[jax.Shape...  54.2 us
    unnamed x16, local copies, waits for them, and re-layouts  3.72 us

profile of v6, /device:TPU:1, one launch (start us, length us, event | category | flops | bytes accessed | tf_op | source)
XLA Modules:
  0.0 121.7 jit_solution(2761015730235569588)
XLA Ops:
  0.6 0.0 copy-start
  0.6 0.0 copy-start.3
  0.7 0.7 copy-done.3
  1.4 0.2 convert_reduce_fusion
  1.6 0.0 copy-start.6
  1.6 0.6 copy-done.6
  2.3 0.7 gather_fusion.1
  2.9 0.7 gather_fusion.3
  3.6 0.1 select_convert_fusion
  3.7 0.0 copy-done
  3.7 0.1 fusion.1
  3.8 0.6 gather_fusion
  4.4 0.1 broadcast_in_dim.94
  4.5 0.1 broadcast_in_dim.95
  4.6 0.0 copy-start.1
  4.6 0.0 copy-start.2
  4.6 0.1 bitcast_select_fusion.refs_2_
  4.7 0.8 copy-done.1
  5.5 0.0 copy-done.2
  5.5 54.2 %shard_map.86 = (f32[16,4096]{1,0:T(8,128)S(1)}, bf16[8,16,4096]{2,1,0:T(8,128)(2,1)S(1)}) custom-call(bf16[128,512]{1,0:T(8,128)(2,1)S(1)} %copy-done.1, bf16[64,512]{1,0:T(8,128)(2,1)S(1)} %bitcast.21, bf16[16,4096]{1,0:T(8,128)(2,1)S(1)} %bitcast_select_fusion.refs_2_), custom_call_target="tpu_custom_call" | custom-call | tf_op jit(solution)/shard_map/pallas_call | solution.py:235
  59.7 0.0 copy-start.5
  59.7 0.0 copy-start.4
  59.7 0.6 gather_fusion.2
  60.4 0.0 copy-done.5
  60.4 0.2 copy-done.4
  60.6 0.2 multiply_reduce_fusion
  60.8 0.1 subtract_convert_fusion
  60.9 59.5 %shard_map.87 = (f32[64,64]{1,0:T(8,128)S(1)}, f32[64,512]{1,0:T(8,128)S(1)}) custom-call(bf16[16,4224]{1,0:T(8,128)(2,1)S(1)} %pad_maximum_fusion.refs_0_), custom_call_target="tpu_custom_call" | custom-call | tf_op jit(solution)/shard_map/pallas_call | solution.py:336
  120.5 0.6 copy.11
  121.1 0.7 copy.12
  (15 shorter events, 0.1 us)
Async XLA Ops:
  0.6 3.1 %copy-start = (bf16[64,4096]{1,0:T(8,128)(2,1)S(1)}, bf16[64,4096]{1,0:T(8,128)(2,1)}, u32[]{:S(2)}) copy-start(bf16[64,4096]{1,0:T(8,128)(2,1)} %param.11) | copy-start | bytes 1572868
  0.6 0.7 copy-start.3
  1.6 0.7 copy-start.6
  4.6 0.9 copy-start.1
  4.6 0.9 copy-start.2
  59.7 0.7 copy-start.5
  59.7 0.9 copy-start.4
